TPU v7x, 32 devices: a whole 2x2x4 slice. The times are simulated.
32 devices in a mesh: dp: 16 (over z, y, x), tensor: 2 (over core).
Axes of the slice: x: 2, y: 2, z: 4, core: 2. Of those that a mesh axis runs over, the one named last changes fastest.
Arguments:
- frames: bfloat16 [2, 32, 512, 512], P(None, ('dp', 'tensor')), may hold values from -6 to 6
- lengths: int32 [2, 32], P(None, 'dp'), may hold values from 128 to 512, as said below
- ffn1_in: bfloat16 [512, 2048], P('dp', 'tensor'), may hold values from -0.25 to 0.25
- ffn1_out: bfloat16 [2048, 512], P('tensor', 'dp'), may hold values from -0.125 to 0.125
- ffn1_bias: bfloat16 [16, 128], P('tensor', 'dp'), may hold values from -3 to 3
- qkv_weight: bfloat16 [512, 3, 512], P('dp', None, 'tensor'), may hold values from -0.25 to 0.25
- pos_weight: bfloat16 [512, 512], P('dp', 'tensor'), may hold values from -0.25 to 0.25
- out_weight: bfloat16 [512, 512], P('tensor', 'dp'), may hold values from -1 to 1
- attn_bias: bfloat16 [4, 4, 128], P(None, 'tensor', 'dp'), may hold values from -3 to 3
- conv_in: bfloat16 [512, 2, 512], P('dp', None, 'tensor'), may hold values from -0.25 to 0.25
- conv_out: bfloat16 [512, 512], P('tensor', 'dp'), may hold values from -0.25 to 0.25
- conv_channel: bfloat16 [13, 4, 128], P(None, 'tensor', 'dp'), may hold values from -2 to 2
- ffn2_in: bfloat16 [512, 2048], P('dp', 'tensor'), may hold values from -0.25 to 0.25
- ffn2_out: bfloat16 [2048, 512], P('tensor', 'dp'), may hold values from -0.125 to 0.125
- ffn2_bias: bfloat16 [16, 128], P('tensor', 'dp'), may hold values from -3 to 3
- norm_params: bfloat16 [14, 512], P(None, ('dp', 'tensor')), may hold values from -1.2 to 1.4
- cotangent: bfloat16 [2, 32, 512, 512], P(None, ('dp', 'tensor')), may hold values from -6 to 6
Outputs:
- activations: bfloat16 [2, 32, 512, 512], P(None, ('dp', 'tensor'))
- frame_grad: bfloat16 [2, 32, 512, 512], P(None, ('dp', 'tensor'))
- ffn1_in_grad: float32 [512, 2048], P('dp', 'tensor')
- ffn1_out_grad: float32 [2048, 512], P('tensor', 'dp')
- ffn1_bias_grad: float32 [16, 128], P('tensor', 'dp')
- qkv_grad: float32 [512, 3, 512], P('dp', None, 'tensor')
- pos_grad: float32 [512, 512], P('dp', 'tensor')
- out_grad: float32 [512, 512], P('tensor', 'dp')
- attn_bias_grad: float32 [4, 4, 128], P(None, 'tensor', 'dp')
- conv_in_grad: float32 [512, 2, 512], P('dp', None, 'tensor')
- conv_out_grad: float32 [512, 512], P('tensor', 'dp')
- conv_channel_grad: float32 [13, 4, 128], P(None, 'tensor', 'dp')
- ffn2_in_grad: float32 [512, 2048], P('dp', 'tensor')
- ffn2_out_grad: float32 [2048, 512], P('tensor', 'dp')
- ffn2_bias_grad: float32 [16, 128], P('tensor', 'dp')
- norm_grad: float32 [14, 512], P(None, ('dp', 'tensor'))
Inputs may be any that keep to these rules, and one draw needn't show every extreme that they name: `lengths`: the last utterance of every micro-batch has 512 frames.
All inputs are finite; a program needn't handle non-finite values.
Results may differ from a plain program's by a relative error of at most 0.04.
Values may be sent and summed in bfloat16 or wider, within the bound.
A program may use at most 256 MiB of HBM per device.

v0:
```python
import math

import jax
import jax.numpy as jnp
from jax import lax
from jax.experimental import pallas as pl
from jax.experimental.pallas import tpu as pltpu
from jax.sharding import PartitionSpec as P

DK = 64
norm_eps = 1e-05
mask_fill = -1000000000.0
BF = jnp.bfloat16
F32 = jnp.float32
BLK = 128


def nn(a, b):
    return lax.dot_general(a, b, (((1,), (0,)), ((), ())), preferred_element_type=F32)


def nt(a, b):
    return lax.dot_general(a, b, (((1,), (1,)), ((), ())), preferred_element_type=F32)


def tn(a, b):
    return lax.dot_general(a, b, (((0,), (0,)), ((), ())), preferred_element_type=F32)


def attn_fwd_kernel(len_ref, qu, qv, k, v, pos, o_ref, lse_ref, u=None, hook=None):
    count = len_ref[pl.program_id(0) if u is None else u]
    full = k.shape[1]
    lane = lax.broadcasted_iota(jnp.int32, (BLK, 2 * DK), 1)
    col = lax.broadcasted_iota(jnp.int32, (BLK, full), 1)
    keep = col < count
    zero = jnp.zeros((), BF)
    for blk in range(full // BLK):
        i0 = blk * BLK
        base = full - BLK - i0
        if hook is not None:
            hook(blk)
        outs, logs = [], []
        for h in range(2):
            mine = (lane < DK) if h == 0 else (lane >= DK)
            q_u = jnp.where(mine, qu[0, i0 : i0 + BLK, :], zero)
            q_v = jnp.where(mine, qv[0, i0 : i0 + BLK, :], zero)
            rel = nt(q_v, pos[base : base + full + BLK, :])
            rel = pltpu.roll(rel, full + 1, 1, stride=1, stride_axis=0)[:, :full]
            s = (nt(q_u, k[0]) + rel) * (1.0 / math.sqrt(DK))
            s = jnp.where(keep, s, mask_fill)
            top = jnp.max(s, axis=1, keepdims=True)
            e = jnp.exp(s - top)
            total = jnp.sum(e, axis=1, keepdims=True)
            outs.append(nn(e.astype(BF), v[0]) / total)
            logs.append(top + jnp.log(total))
        left = lane < DK
        o_ref[0, i0 : i0 + BLK, :] = jnp.where(left, outs[0], outs[1]).astype(BF)
        lse_ref[0, i0 : i0 + BLK, :] = jnp.where(left, logs[0], logs[1])


def attn_bwd_kernel(
    len_ref, qu, qv, k, v, pos, o, lse, do, dq_ref, dk_ref, dv_ref, dpos_ref, sum_ref, dkt, dvt, dpt,
    hook=None,
):
    count = len_ref[pl.program_id(0)]
    full = k.shape[1]
    scale = 1.0 / math.sqrt(DK)
    lane = lax.broadcasted_iota(jnp.int32, (BLK, 2 * DK), 1)
    left = lane < DK
    keep = lax.broadcasted_iota(jnp.int32, (BLK, full), 1) < count
    zero = jnp.zeros((), BF)
    flip = (lane + lax.broadcasted_iota(jnp.int32, (BLK, 2 * DK), 0) == BLK - 1).astype(F32).astype(BF)
    dkt[...] = jnp.zeros_like(dkt)
    dvt[...] = jnp.zeros_like(dvt)
    dpt[...] = jnp.zeros_like(dpt)
    sum_q = jnp.zeros((1, 2 * DK), F32)
    sum_u = jnp.zeros((1, 2 * DK), F32)
    sum_v = jnp.zeros((1, 2 * DK), F32)
    for blk in range(full // BLK):
        i0 = blk * BLK
        base = full - BLK - i0
        rows = slice(i0, i0 + BLK)
        win = slice(base, base + full + BLK)
        if hook is not None:
            hook(blk)
        qu_t = qu[0, rows, :].astype(F32).T.astype(BF)
        do_t = do[0, rows, :].astype(F32).T.astype(BF)
        qv_t = tn(qv[0, rows, :], flip).astype(BF)
        dot_o = do[0, rows, :].astype(F32) * o[0, rows, :].astype(F32)
        parts_u, parts_v = [], []
        for h in range(2):
            mine = left if h == 0 else lane >= DK
            hs = slice(h * DK, h * DK + DK)
            q_u = jnp.where(mine, qu[0, rows, :], zero)
            q_v = jnp.where(mine, qv[0, rows, :], zero)
            d_o = jnp.where(mine, do[0, rows, :], zero)
            rel = nt(q_v, pos[win, :])
            rel = pltpu.roll(rel, full + 1, 1, stride=1, stride_axis=0)[:, :full]
            s = (nt(q_u, k[0]) + rel) * scale - lse[0, rows, h * DK : h * DK + 1]
            p = jnp.where(keep, jnp.exp(jnp.minimum(s, 0.0)), 0.0)
            delta = jnp.sum(jnp.where(mine, dot_o, 0.0), axis=1, keepdims=True)
            ds = (p * (nt(d_o, v[0]) - delta)).astype(BF)
            dvt[hs, :] += nn(do_t[hs, :], p.astype(BF))
            dkt[hs, :] += nn(qu_t[hs, :], ds)
            parts_u.append(nn(ds, k[0]))
            wide = jnp.concatenate([nn(flip, ds), jnp.zeros((BLK, BLK), F32)], axis=1)
            wide = pltpu.roll(wide, 0, 1, stride=1, stride_axis=0).astype(BF)
            parts_v.append(nn(wide, pos[win, :]))
            dpt[hs, win] += nn(qv_t[hs, :], wide)
        d_u = jnp.where(left, parts_u[0], parts_u[1]) * scale
        d_v = jnp.where(left, parts_v[0], parts_v[1]) * scale
        high = d_v.astype(BF)
        low = (d_v - high.astype(F32)).astype(BF)
        d_q = (d_u + nn(flip, high) + nn(flip, low)).astype(BF)
        dq_ref[0, rows, :] = d_q
        sum_q += jnp.sum(d_q.astype(F32), axis=0, keepdims=True)
        sum_u += jnp.sum(d_u, axis=0, keepdims=True)
        sum_v += jnp.sum(d_v, axis=0, keepdims=True)
    dk_ref[0] = (dkt[...].T * scale).astype(BF)
    d_val = dvt[...].T.astype(BF)
    dv_ref[0] = d_val
    dpos_ref[0] = (dpt[...].T * scale).astype(BF)
    sum_ref[0, 0:1, :] = sum_q
    sum_ref[0, 1:2, :] = jnp.sum(d_val.astype(F32), axis=0, keepdims=True)
    sum_ref[0, 2:3, :] = sum_u
    sum_ref[0, 3:4, :] = sum_v
    sum_ref[0, 4:8, :] = jnp.zeros((4, 2 * DK), F32)


def attn_specs(rows, full, width):
    pairs = width // (2 * DK)
    main = pl.BlockSpec((1, full, 2 * DK), lambda u, p, n: (u, 0, p))
    pos = pl.BlockSpec((2 * full, 2 * DK), lambda u, p, n: (0, p))
    return (rows, pairs), main, pos


def attn_fwd_call(lens, qu, qv, k, v, pos):
    rows, full, width = qu.shape
    grid, main, pspec = attn_specs(rows, full, width)
    return pl.pallas_call(
        attn_fwd_kernel,
        grid_spec=pltpu.PrefetchScalarGridSpec(
            num_scalar_prefetch=1,
            grid=grid,
            in_specs=[main] * 4 + [pspec],
            out_specs=[main, main],
        ),
        out_shape=[
            jax.ShapeDtypeStruct((rows, full, width), BF),
            jax.ShapeDtypeStruct((rows, full, width), F32),
        ],
        compiler_params=dense_params(),
        name="attn_fwd",
    )(lens, qu, qv, k, v, pos)


def attn_bwd_call(lens, qu, qv, k, v, pos, o, lse, do, early=None, cid=None):
    rows, full, width = qu.shape
    grid, main, pspec = attn_specs(rows, full, width)
    args = [lens, qu, qv, k, v, pos, o, lse, do]
    in_specs = [main] * 4 + [pspec] + [main] * 3
    out_specs = [
        main,
        main,
        main,
        pl.BlockSpec((1, 2 * full, 2 * DK), lambda u, p, n: (u, 0, p)),
        pl.BlockSpec((1, 8, 2 * DK), lambda u, p, n: (u, 0, p)),
    ]
    scratch = [
        pltpu.VMEM((2 * DK, full), F32),
        pltpu.VMEM((2 * DK, full), F32),
        pltpu.VMEM((2 * DK, 2 * full), F32),
    ]
    out_shape = [jax.ShapeDtypeStruct((rows, full, width), BF)] * 3 + [
        jax.ShapeDtypeStruct((rows, 2 * full, width), BF),
        jax.ShapeDtypeStruct((rows, 8, width), F32),
    ]
    body, params = attn_bwd_kernel, dense_params()
    if early is not None:
        items = [split_owners(item) for item in early]
        pieces = pieces_of([item.shape[-1] for item in items])
        owned = items[0].shape[-2]
        n_in, n_out, m = len(args) - 1, len(out_shape), len(items)
        args += items
        in_specs += [ANY] * m
        out_specs.append(pl.BlockSpec((owned, C_OWN), lambda u, p, n: (0, 0)))
        out_shape.append(jax.ShapeDtypeStruct((owned, C_OWN), F32))
        scratch += scatter_scratch(pieces, owned)
        params = comm_params(cid)

        def body(*refs):
            at = pl.program_id(0) * grid[1] + pl.program_id(1)
            last = grid[0] * grid[1] - 1
            ins, rest = refs[: 1 + n_in], refs[1 + n_in :]
            g_refs, rest = rest[:m], rest[m:]
            mains, o_ref, rest = rest[:n_out], rest[n_out], rest[n_out + 1 :]
            own, sems = rest[:3], rest[3:]
            start, advance, finish, rounds = scatter_steps(pieces, g_refs, o_ref, sems, 2)
            peers = link_peers(*place())

            @pl.when(at == 0)
            def _():
                hail(peers)

            def begin():
                hear(peers)
                for p in range(len(pieces)):
                    start(p)

            steps = [begin] + [lambda q=q: advance(q) for q in range(rounds)]
            attn_bwd_kernel(*ins, *mains, *own, hook=hooks_of(steps, at, last, full // BLK))

            @pl.when(at == last)
            def _():
                finish()

    return pl.pallas_call(
        body,
        grid_spec=pltpu.PrefetchScalarGridSpec(
            num_scalar_prefetch=1,
            grid=grid,
            in_specs=in_specs,
            out_specs=out_specs,
            scratch_shapes=scratch,
        ),
        out_shape=out_shape,
        compiler_params=params,
        name="attn_bwd",
    )(*args)


def hooks_of(steps, at, last, spots):
    def hook(blk):
        for i, step in enumerate(steps):
            where, spot = divmod(i * (last + 1) * (spots - 1) // len(steps), spots - 1)
            if spot + 1 == blk:

                @pl.when(at == where)
                def _(step=step):
                    step()

    return hook


MESH = pl.DeviceIdType.MESH
NZ, NY, NX = 4, 2, 2
ANY = pl.BlockSpec(memory_space=pl.ANY)
VM = pl.BlockSpec(memory_space=pltpu.VMEM)


def own_mesh(sizes):
    return sizes == (NZ * NY * NX, 2)


def place():
    dp = lax.axis_index("dp")
    return dp // (NY * NX), dp // NX % NY, dp % NX, lax.axis_index("tensor")


def dev(z, y, x, t):
    return (z * (NY * NX) + y * NX + x, t)


def hail(peers):
    barrier = pltpu.get_barrier_semaphore()
    for peer in peers:
        pl.semaphore_signal(barrier, inc=1, device_id=peer, device_id_type=MESH)


def hear(peers):
    pl.semaphore_wait(pltpu.get_barrier_semaphore(), len(peers))


def rcopy(src, dst, send, recv, peer):
    return pltpu.make_async_remote_copy(
        src_ref=src, dst_ref=dst, send_sem=send, recv_sem=recv, device_id=peer, device_id_type=MESH
    )


def link_peers(z, y, x, t):
    peers = [dev(lax.rem(z + d, NZ), y, x, t) for d in range(1, NZ)]
    return peers + [dev(z, 1 - y, x, t), dev(z, y, 1 - x, t), dev(z, y, x, 1 - t)]


def sum_scratch(shape):
    dma = pltpu.SemaphoreType.DMA
    return [
        pltpu.VMEM(shape, F32), pltpu.VMEM(shape, F32), pltpu.VMEM((3,) + shape, F32),
        pltpu.VMEM((7,) + shape, F32), dma((3,)), dma((3,)), dma((7,)), dma((7,)),
    ]


def sum_steps(scratch):
    x_s, mid, b1, b2, s1, r1, s2, r2 = scratch
    z, y, x, t = place()
    spot = (y * NX + x) * 2 + t
    zs = [dev(lax.rem(z + d, NZ), y, x, t) for d in range(1, NZ)]
    flat = [lax.rem(spot + d, 8) for d in range(1, 8)]
    plane = [dev(z, p // 4, p // 2 % 2, p % 2) for p in flat]

    def call(wait=False):
        hear(zs + plane) if wait else hail(zs + plane)

    def meet(o_ref, heard=False):
        first = [rcopy(x_s, b1.at[i], s1.at[i], r1.at[i], peer) for i, peer in enumerate(zs)]
        second = [rcopy(mid, b2.at[i], s2.at[i], r2.at[i], peer) for i, peer in enumerate(plane)]

        def one():
            if not heard:
                hear(zs + plane)
            for copy in first:
                copy.start()

        def two():
            for copy in first:
                copy.wait_recv()
            mid[...] = (x_s[...] + b1[0]) + (b1[1] + b1[2])
            for copy in second:
                copy.start()

        def three():
            for copy in second:
                copy.wait_recv()
            total = mid[...]
            for i in range(7):
                total = total + b2[i]
            o_ref[...] = total
            for copy in first + second:
                copy.wait_send()

        return one, two, three

    return call, meet


def comm_params(cid):
    return pltpu.CompilerParams(
        collective_id=cid, has_side_effects=True, vmem_limit_bytes=60 * 1024 * 1024
    )


def gathered_shape(packed):
    return jax.ShapeDtypeStruct((2, NZ, NY, NX) + packed.shape, packed.dtype)


def gather_scratch(n, groups=3):
    dma = pltpu.SemaphoreType.DMA
    return [dma((n, NZ - 1)), dma((n, NZ - 1))] + [dma((n,))] * 6 + [dma((groups,))]


LEAD = 3


def gather_events(pieces, xs, gs, sems):
    zs, zr, as_, ar, bs, br, cs, cr, own_sem = sems
    z, y, x, t = place()
    along_x, along_y = dev(z, y, 1 - x, t), dev(z, 1 - y, x, t)
    zc, ac, bc, cc = [], [], [], []
    for p, (i, start, w) in enumerate(pieces):
        c = pl.ds(start, w)
        g = gs[i]
        zc.append(
            [
                rcopy(
                    xs[i].at[:, c],
                    g.at[t, z, y, x, :, c],
                    zs.at[p, d - 1],
                    zr.at[p, d - 1],
                    dev(lax.rem(z + d, NZ), y, x, t),
                )
                for d in range(1, NZ)
            ]
        )
        line = g.at[t, :, y, x, :, c]
        ac.append(rcopy(line, line, as_.at[p], ar.at[p], along_x if p % 2 == 0 else along_y))
        half = g.at[t, :, y, :, :, c] if p % 2 == 0 else g.at[t, :, :, x, :, c]
        bc.append(rcopy(half, half, bs.at[p], br.at[p], along_y if p % 2 == 0 else along_x))
        full = g.at[t, :, :, :, :, c]
        cc.append(rcopy(full, full, cs.at[p], cr.at[p], dev(z, y, x, 1 - t)))

    def begin():
        own = [
            pltpu.make_async_copy(item, g.at[t, z, y, x], own_sem.at[i])
            for i, (item, g) in enumerate(zip(xs, gs))
        ]
        for copy in own:
            copy.start()
        for copies in zc[: 2 * LEAD]:
            for copy in copies:
                copy.start()
        for copy in own:
            copy.wait()

    def event(kind, q):
        for p in (2 * q, 2 * q + 1):
            if kind == "z":
                for copy in zc[p]:
                    copy.wait_recv()
                ac[p].start()
                for copy in zc[p + 2 * LEAD] if p + 2 * LEAD < len(pieces) else []:
                    copy.start()
            elif kind == "a":
                ac[p].wait_recv()
                bc[p].start()
            elif kind == "b":
                bc[p].wait_recv()
                cc[p].start()
            else:
                cc[p].wait_recv()

    def finish():
        for copy in sum(zc, []) + ac + bc + cc:
            copy.wait_send()

    return begin, event, finish


def gather_order(pieces):
    unit = [0.42 * (pieces[2 * q][2] + pieces[2 * q + 1][2]) / 512 for q in range(len(pieces) // 2)]
    order, at = [], 3.0
    waiting = []
    for q, step in enumerate(unit):
        at += 8 * step
        waiting.append((at + 2.5, q, "z"))
    free = 0.0
    while waiting:
        waiting.sort()
        now, q, kind = waiting.pop(0)
        order.append((now, kind, q))
        if kind in "za":
            free = max(free, now) + (4 if kind == "z" else 8) * unit[q]
            waiting.append((free + 2.5, q, "a" if kind == "z" else "b"))
        elif kind == "b":
            waiting.append((now + 1.8, q, "c"))
    return order


def small_steps(s_ref, v_ref, mid, b1, b2, s1, r1, s2, r2):
    z, y, x, t = place()
    spot = (y * NX + x) * 2 + t
    zs = [dev(lax.rem(z + d, NZ), y, x, t) for d in range(1, NZ)]
    flat = [lax.rem(spot + d, 8) for d in range(1, 8)]
    plane = [dev(z, p // 4, p // 2 % 2, p % 2) for p in flat]
    first = [rcopy(s_ref, b1.at[i], s1.at[i], r1.at[i], peer) for i, peer in enumerate(zs)]
    second = [rcopy(mid, b2.at[i], s2.at[i], r2.at[i], peer) for i, peer in enumerate(plane)]

    def begin():
        for copy in first:
            copy.start()

    def spread():
        for copy in first:
            copy.wait_recv()
        mid[...] = (s_ref[...] + b1[0]) + (b1[1] + b1[2])
        for copy in second:
            copy.start()

    def finish():
        for copy in second:
            copy.wait_recv()
        same, other = mid[...].astype(F32), b2[0].astype(F32)
        for i in range(1, 7):
            if i % 2 == 1:
                same = same + b2[i].astype(F32)
            else:
                other = other + b2[i].astype(F32)
        low = jnp.where(t == 0, same, other)
        high = jnp.where(t == 0, other, same)
        v_ref[...] = jnp.zeros_like(v_ref)
        for q in range(4):
            r = S_NORM + 14 * q
            v_ref[0:14, 128 * q : 128 * q + 128] = low[r : r + 14] + high[r : r + 14]
        for i, part in enumerate((low, high)):
            for q in range(2):
                c = slice((2 * i + q) * 128, (2 * i + q) * 128 + 128)
                v_ref[R_ATT:R_CV, c] = part[S_ATT + 4 * q : S_ATT + 4 * q + 4]
                v_ref[R_CV:R_B1, c] = part[S_CV + 13 * q : S_CV + 13 * q + 13]
            for q in range(8):
                r, c = 2 * i + q // 4, slice(q % 4 * 128, q % 4 * 128 + 128)
                v_ref[R_B1 + r : R_B1 + r + 1, c] = part[S_B1 + q : S_B1 + q + 1]
                v_ref[R_B2 + r : R_B2 + r + 1, c] = part[S_B2 + q : S_B2 + q + 1]
        for copy in first + second:
            copy.wait_send()

    return plane, begin, spread, finish


S_B1, S_ATT, S_CV, S_B2, S_NORM, S_ALL = 0, 8, 16, 42, 50, 112


def lanes_of(n, offset):
    at = lax.broadcasted_iota(jnp.int32, (n, 128), 0) + offset
    return (lax.broadcasted_iota(jnp.int32, (n, 128), 1) == at).astype(F32)


def prep_kernel(
    f1i, f1o, pos, qkv, f2i, f2o, ci, out, co, b1, att, cv, b2, norm,
    pa_ref, pb_ref, pc_ref, slab_ref, table_ref, slab, first_s, second_s,
):
    def put(ref, name, value, shift=0):
        start = SEG[name][0] + shift
        ref[:, start : start + value.shape[1]] = value

    for ref, name, item in (
        (pa_ref, "f1i", f1i), (pa_ref, "f1o", f1o), (pa_ref, "pos", pos), (pc_ref, "f2i", f2i),
        (pc_ref, "f2o", f2o), (pb_ref, "out", out), (pb_ref, "co", co),
    ):
        put(ref, name, item[...])
    for k in range(3):
        put(pa_ref, "qkv", qkv[k], k * qkv.shape[2])
    for k in range(2):
        put(pb_ref, "ci", ci[:, k, :], k * ci.shape[2])
    z, y, x, t = place()
    dp = z * (NY * NX) + y * NX + x
    sel = lanes_of(8, dp * 8).astype(BF)
    slab[...] = jnp.zeros_like(slab)
    slab[S_B1 : S_B1 + 8] = nn(b1[...], sel)
    for q in range(2):
        slab[S_ATT + 4 * q : S_ATT + 4 * q + 4] = nn(att[:, q, :], sel)
        slab[S_CV + 13 * q : S_CV + 13 * q + 13] = tn(cv[q], sel)
    slab[S_B2 : S_B2 + 8] = nn(b2[...], sel)
    at = dp * 2 + t
    here = nn(norm[...], lanes_of(16, lax.rem(at, 8) * 16).astype(BF))
    for q in range(4):
        slab[S_NORM + 14 * q : S_NORM + 14 * q + 14] = here * (at // 8 == q).astype(F32)
    slab_ref[...] = slab[...].astype(BF)
    fill_table(table_ref, first_s, second_s)


def prep_call(items, smalls, full, width):
    rows = items[0].shape[0]
    return pl.pallas_call(
        prep_kernel,
        in_specs=[VM] * 14,
        out_specs=[VM] * 5,
        out_shape=[
            jax.ShapeDtypeStruct((rows, C_A), BF),
            jax.ShapeDtypeStruct((rows, C_B), BF),
            jax.ShapeDtypeStruct((rows, C_C), BF),
            jax.ShapeDtypeStruct((S_ALL, 128), BF),
            jax.ShapeDtypeStruct((2 * full, width), BF),
        ],
        scratch_shapes=[pltpu.VMEM((S_ALL, 128), F32)] + [pltpu.VMEM((32, width), F32)] * 2,
        name="prepare",
    )(*items, *smalls)


def split_owners(item):
    return item.reshape(2, NZ, NY, NX, item.shape[1] // (NZ * NY * NX), item.shape[2])


def pieces_of(widths, step=256):
    pieces, at = [], 0
    for i, w in enumerate(widths):
        pieces += [(i, k, min(step, w), at + k) for k in range(0, w, step)]
        at += w
    return pieces


def scatter_scratch(pieces, rows):
    n = len(pieces)
    total = sum(piece[2] for piece in pieces)
    dma = pltpu.SemaphoreType.DMA
    shape = (rows, total)
    return [
        pltpu.VMEM((NZ, NY, NX) + shape, BF),
        pltpu.VMEM((NZ, NY, NX) + shape, BF),
        pltpu.VMEM((NZ, 2) + shape, BF),
        pltpu.VMEM((NZ,) + shape, BF),
        pltpu.VMEM((NZ - 1,) + shape, BF),
    ] + [dma((n,))] * 7 + [dma((n, NZ - 1))] * 2


def scatter_steps(pieces, g_refs, o_ref, scratch, lag):
    own, rc, ra, rb, rz, lsem, cs, cr, as_, ar, bs, br, zs, zr = scratch
    z, y, x, t = place()
    along_x, along_y = dev(z, y, 1 - x, t), dev(z, 1 - y, x, t)
    mate = dev(z, y, x, 1 - t)
    count = len(pieces)
    bufs, lc, cc, ac, bc, zc = [], [], [], [], [], []
    for p, (i, start, w, at) in enumerate(pieces):
        c = pl.ds(at, w)
        g = pl.ds(start, w)
        b = dict(
            own=own.at[:, :, :, :, c], rc=rc.at[:, :, :, :, c], ra=ra.at[:, :, :, c],
            rb=rb.at[:, :, c], rz=rz.at[:, :, c],
        )
        bufs.append(b)
        even = p % 2 == 0
        lc.append(
            pltpu.make_async_copy(g_refs[i].at[t, :, :, :, :, g], b["own"], lsem.at[p])
        )
        cc.append(rcopy(g_refs[i].at[1 - t, :, :, :, :, g], b["rc"], cs.at[p], cr.at[p], mate))
        away = b["own"].at[:, 1 - y] if even else b["own"].at[:, :, 1 - x]
        ac.append(rcopy(away, b["ra"], as_.at[p], ar.at[p], along_y if even else along_x))
        line = b["own"].at[:, y, 1 - x] if even else b["own"].at[:, 1 - y, x]
        bc.append(rcopy(line, b["rb"], bs.at[p], br.at[p], along_x if even else along_y))
        zc.append([])
        for d in range(1, NZ):
            far = lax.rem(z + d, NZ)
            zc[p].append(
                rcopy(
                    b["own"].at[far, y, x], b["rz"].at[d - 1], zs.at[p, d - 1], zr.at[p, d - 1],
                    dev(far, y, x, t),
                )
            )

    def start(p):
        lc[p].start()
        cc[p].start()

    def advance(q):
        if q < count:
            lc[q].wait()
            cc[q].wait_recv()
            b = bufs[q]

            @pl.loop(0, NZ)
            def _(i):
                b["own"][i] = b["own"][i] + b["rc"][i]

            ac[q].start()
        p = q - lag
        if 0 <= p < count:
            ac[p].wait_recv()
            b = bufs[p]

            @pl.loop(0, NZ)
            def _(i):
                if p % 2 == 0:
                    b["own"][i, y] = b["own"][i, y] + b["ra"][i]
                else:
                    b["own"][i, :, x] = b["own"][i, :, x] + b["ra"][i]

            bc[p].start()
        p = q - 2 * lag
        if 0 <= p < count:
            bc[p].wait_recv()
            b = bufs[p]

            @pl.loop(0, NZ)
            def _(i):
                b["own"][i, y, x] = b["own"][i, y, x] + b["rb"][i]

            for copy in zc[p]:
                copy.start()
        p = q - 3 * lag
        if 0 <= p < count:
            for copy in zc[p]:
                copy.wait_recv()
            b = bufs[p]
            total = b["own"][z, y, x].astype(F32)
            for d in range(NZ - 1):
                total = total + b["rz"][d].astype(F32)
            o_ref[:, pieces[p][3] : pieces[p][3] + pieces[p][2]] = total

    def finish():
        for copy in cc + ac + bc + sum(zc, []):
            copy.wait_send()

    return start, advance, finish, count + 3 * lag


def small_sum_steps(parts, ext, scratch):
    acc_s, bc_, bz, bp, bm, sc, rc, sz, rz, sp, rp, sm, rm = scratch
    z, y, x, t = place()
    dp = z * (NY * NX) + y * NX + x
    half = acc_s.shape[0] // 2
    mine = pl.ds(pl.multiple_of(t * half, 8), half)
    mate = dev(z, y, x, 1 - t)
    spot = y * NX + x
    zp = [dev(lax.rem(z + d, NZ), y, x, t) for d in range(1, NZ)]
    flat = [lax.rem(spot + d, 4) for d in range(1, 4)]
    pp = [dev(z, p // 2, p % 2, t) for p in flat]
    one = rcopy(acc_s, bc_, sc, rc, mate)
    two = [rcopy(acc_s.at[mine], bz.at[i], sz.at[i], rz.at[i], peer) for i, peer in enumerate(zp)]
    three = [rcopy(bz.at[3], bp.at[i], sp.at[i], rp.at[i], peer) for i, peer in enumerate(pp)]
    four = rcopy(bp.at[3], bm, sm, rm, mate)

    def a():
        acc_s[...] = jnp.zeros_like(acc_s)
        total = parts[0][...]
        for part in parts[1:]:
            total = total + part[...]
        acc_s[0:R_ALL] = total
        one.start()

    def b():
        one.wait()
        acc_s[...] = acc_s[...] + bc_[...]
        for copy in two:
            copy.start()

    def c():
        for copy in two:
            copy.wait()
        bz[3] = (acc_s[mine] + bz[0]) + (bz[1] + bz[2])
        for copy in three:
            copy.start()

    def d():
        for copy in three:
            copy.wait()
        bp[3] = (bz[3] + bp[0]) + (bp[1] + bp[2])
        four.start()
        ext[mine] = bp[3]

    def e():
        four.wait()
        ext[pl.ds(pl.multiple_of((1 - t) * half, 8), half)] = bm[...]

    return pp, [a, b, c, d, e]


def small_sum_scratch(width):
    dma = pltpu.SemaphoreType.DMA
    return [
        pltpu.VMEM((R_SUM, width), F32), pltpu.VMEM((R_SUM, width), F32),
        pltpu.VMEM((4, R_SUM // 2, width), F32), pltpu.VMEM((4, R_SUM // 2, width), F32),
        pltpu.VMEM((R_SUM // 2, width), F32), dma, dma, dma((3,)), dma((3,)), dma((3,)), dma((3,)), dma, dma,
    ]


def finish_kernel(
    oa, ob, ext, f1i, f1o, b1, qkv, pos, out, att, ci, co, cv, f2i, f2o, b2, norm
):
    def take(ref, name):
        start = OWN.get(name, SEG[name][0])
        return ref[:, start : start + SEG[name][1]]

    f1i[...] = take(oa, "f1i")
    f1o[...] = take(oa, "f1o")
    pos[...] = take(oa, "pos")
    f2i[...] = take(ob, "f2i")
    f2o[...] = take(ob, "f2o")
    out[...] = take(ob, "out")
    co[...] = take(ob, "co")
    for ref, src, name in ((qkv, oa, "qkv"), (ci, ob, "ci")):
        start, w = OWN.get(name, SEG[name][0]), SEG[name][1]
        n = 3 if name == "qkv" else 2
        for k in range(n):
            part = src[:, start + k * w // n : start + (k + 1) * w // n]
            if name == "qkv":
                ref[k] = part
            else:
                ref[:, k, :] = part
    z, y, x, t = place()
    dp = z * (NY * NX) + y * NX + x
    sel = lanes_of(8, dp * 8)

    def own(v, pick):
        return lax.dot_general(
            v, pick, (((1,), (1,)), ((), ())), precision=lax.Precision.HIGHEST,
            preferred_element_type=F32,
        )

    for q in range(2):
        c = pl.ds(pl.multiple_of((2 * t + q) * 128, 128), 128)
        att[:, q, :] = own(ext[R_ATT:R_CV, c], sel)
        cv[q] = own(sel, ext[R_CV:R_B1, c])
    for o, at in ((b1, R_B1), (b2, R_B2)):
        for q in range(8):
            r, c = at + q // 4, slice(q % 4 * 128, q % 4 * 128 + 128)
            line = jnp.where(t == 0, ext[r : r + 1, c], ext[r + 2 : r + 3, c])
            o[q : q + 1, :] = own(line, sel)
    at = dp * 2 + t
    lane = pl.ds(pl.multiple_of(at // 8 * 128, 128), 128)
    norm[...] = own(ext[0:14, lane], lanes_of(16, lax.rem(at, 8) * 16))


def finish_call(oa, ob, ext, rows):
    shapes = [
        (rows, 1024), (rows, 1024), (8, 8), (3, rows, 256), (rows, 256), (rows, 256), (4, 2, 8),
        (rows, 2, 256), (rows, 256), (2, 8, 13), (rows, 1024), (rows, 1024), (8, 8), (14, 16),
    ]
    f1i, f1o, b1, qkv, pos, out, att, ci, co, cv, f2i, f2o, b2, norm = pl.pallas_call(
        finish_kernel,
        in_specs=[VM] * 3,
        out_specs=[VM] * 14,
        out_shape=[jax.ShapeDtypeStruct(shape, F32) for shape in shapes],
        name="own_gradients",
    )(oa, ob, ext)
    return (
        f1i, f1o.T, b1, qkv.transpose(1, 0, 2), pos, out.T, att, ci, co.T, cv.transpose(2, 0, 1),
        f2i, f2o.T, b2, norm,
    )

SEG = {
    "f1i": (0, 1024), "f1o": (1024, 1024), "pos": (2048, 256), "qkv": (2304, 768),
    "ci": (0, 512), "out": (512, 256), "co": (768, 256),
    "f2i": (0, 1024), "f2o": (1024, 1024),
}
C_A, C_B, C_C = 3072, 1024, 2048
OWN = {"f2i": 0, "f2o": 1024, "ci": 2048, "out": 2560, "co": 2816}
C_OWN = 3072
R_ATT, R_CV, R_B1, R_B2, R_ALL, R_SUM = 14, 18, 31, 35, 40, 48
TB = 256
HC = 256


def seg_spec(name, depth):
    start, width = SEG[name]
    return pl.BlockSpec(
        (2, depth, width), lambda i, *_: (0, 0, start // width), pipeline_mode=pl.Buffered(1)
    )


def whole(shape):
    zeros = (0,) * len(shape)
    return pl.BlockSpec(shape, lambda i, *_: zeros)


def tall(rows, width):
    return pl.BlockSpec((rows, width), lambda i, *_: (i, 0))


def sig(v):
    return 0.5 * jnp.tanh(0.5 * v) + 0.5


def row(ref, i):
    return ref[i : i + 1, :]


def col_sum(v):
    return jnp.sum(v, axis=0, keepdims=True)


def ln_stats(v):
    centered = v - jnp.mean(v, axis=1, keepdims=True)
    inv = lax.rsqrt(jnp.mean(centered * centered, axis=1, keepdims=True) + norm_eps)
    return centered * inv, inv


def ln_back(up, scaled, inv, gain):
    g = up * gain
    return inv * (
        g
        - jnp.mean(g, axis=1, keepdims=True)
        - scaled * jnp.mean(g * scaled, axis=1, keepdims=True)
    )


def bias_half(vecs, at, t):
    return jnp.concatenate([row(vecs, at + 2 * t), row(vecs, at + 2 * t + 1)], axis=1)


def row_mask(start, rows, count):
    at = start + lax.broadcasted_iota(jnp.int32, (rows, 1), 0)
    return (at < count).astype(F32)


def ffn1_kernel(
    x_ref, table, w_in, w_out, w_qkv, w_pos, vecs,
    first_ref, z_ref, qu_ref, qv_ref, k_ref, v_ref, pos_ref,
):
    x = x_ref[...].astype(F32)
    scaled, _ = ln_stats(x)
    hn = (scaled * row(vecs, 0) + row(vecs, 1)).astype(BF)
    half = w_in.shape[2]
    y = row(vecs, 2)
    for t in range(2):
        z = nn(hn, w_in[t]) + bias_half(vecs, R_B1, t)
        for j in range(half // HC):
            z_ref[:, (2 * j + t) * HC : (2 * j + t + 1) * HC] = z[:, j * HC : (j + 1) * HC].astype(BF)
        y = y + nt((z * sig(z)).astype(BF), w_out[t])
    first = x + 0.5 * y
    first_ref[...] = first
    scaled, _ = ln_stats(first)
    hn = (scaled * row(vecs, 3) + row(vecs, 4)).astype(BF)
    part = w_qkv.shape[2] // 3
    for t in range(2):
        c = slice(t * part, (t + 1) * part)
        proj = nn(hn, w_qkv[t])
        q = proj[:, :part] + vecs[R_ATT : R_ATT + 1, c]
        qu_ref[:, c] = (q + vecs[R_ATT + 2 : R_ATT + 3, c]).astype(BF)
        qv_ref[:, c] = (q + vecs[R_ATT + 3 : R_ATT + 4, c]).astype(BF)
        k_ref[:, c] = proj[:, part : 2 * part].astype(BF)
        v_ref[:, c] = (proj[:, 2 * part :] + vecs[R_ATT + 1 : R_ATT + 2, c]).astype(BF)
        pos_ref[:, c] = nn(table[...], w_pos[t]).astype(BF)


def dense_params(mib=60):
    return pltpu.CompilerParams(vmem_limit_bytes=mib * 1024 * 1024)


def ffn1_call(x, table, g, vecs):
    tokens, width = x.shape
    steps = tokens // TB
    places = tall(table.shape[0] // steps, width)
    return pl.pallas_call(
        ffn1_kernel,
        grid=(steps,),
        in_specs=[
            tall(TB, width), places, seg_spec("f1i", width), seg_spec("f1o", width),
            seg_spec("qkv", width), seg_spec("pos", width), whole(vecs.shape),
        ],
        out_specs=[tall(TB, width), tall(TB, 4 * width)] + [tall(TB, width)] * 4 + [places],
        out_shape=[
            jax.ShapeDtypeStruct((tokens, width), F32),
            jax.ShapeDtypeStruct((tokens, 4 * width), BF),
        ]
        + [jax.ShapeDtypeStruct((tokens, width), BF)] * 4
        + [jax.ShapeDtypeStruct(table.shape, BF)],
        compiler_params=dense_params(),
        name="ffn1_forward",
    )(x, table, g, g, g, g, vecs)


FRONT_PIECES = (
    [(0, at + 256 * j, 256) for j in range(4) for at in (0, 1024)]
    + [(0, 2048 + 256 * k, 256) for k in range(4)]
    + [(1, 256 * k, 256) for k in (2, 0, 1, 3)]
    + [(2, at + 256 * j, 256) for j in range(4) for at in (0, 1024)]
)


def front_call(lens, x, table, packed_a, packed_b, packed_c, slab, batch, cid):
    tokens, width = x.shape
    full = tokens // batch
    pairs = width // (2 * DK)
    chunks = SEG["f1i"][1] // HC
    first_head = chunks + 1
    steps = first_head + batch * pairs
    order = gather_order(FRONT_PIECES)
    dma = pltpu.SemaphoreType.DMA
    small = [
        pltpu.VMEM(slab.shape, BF), pltpu.VMEM((3,) + slab.shape, BF),
        pltpu.VMEM((7,) + slab.shape, BF), dma((3,)), dma((3,)), dma((7,)), dma((7,)),
    ]
    heads_shape = (batch, full, width)
    scratch = [
        pltpu.VMEM((2, NZ, NY, NX) + packed_a.shape, BF),
        pltpu.VMEM((tokens, width), F32),
        pltpu.VMEM((tokens, width), BF),
    ]
    scratch += [pltpu.VMEM(heads_shape, BF)] * 5 + [pltpu.VMEM(heads_shape, F32)]
    scratch += [pltpu.VMEM(table.shape, BF), dma((10,))]
    n_own = len(scratch)

    def body(
        len_ref, x_ref, table_ref, xa_ref, xb_ref, xc_ref, s_ref,
        ga_ref, gb_ref, gc_ref, vecs, first_ref, z_ref, qu_ref, qv_ref, k_ref, v_ref, pos_ref, mix_ref,
        lse_ref, *rest,
    ):
        i = pl.program_id(0)
        ga, y_s, hn_s, qu, qv, k, v, mix, lse, pos, out_sem = rest[:n_own]
        smalls = rest[n_own : n_own + len(small)]
        begin, event, finish = gather_events(
            FRONT_PIECES, (xa_ref, xb_ref, xc_ref), (ga, gb_ref, gc_ref), rest[n_own + len(small) :]
        )
        plane, s_begin, s_spread, s_finish = small_steps(s_ref, vecs, *smalls)
        z, y, xx, t = place()
        sources = (ga, y_s, qu, qv, k, v, pos, mix, lse)
        targets = (ga_ref, first_ref, qu_ref, qv_ref, k_ref, v_ref, pos_ref, mix_ref, lse_ref)
        copies = [
            pltpu.make_async_copy(a, b, out_sem.at[n])
            for n, (a, b) in enumerate(zip(sources, targets))
        ]
        done = [0]

        def until(q):
            while True:
                _, kind, pair = order[done[0]]
                done[0] += 1
                event(kind, pair)
                if (kind, pair) == ("c", q):
                    break

        def weight(t, start, w):
            return ga[t, :, :, :, :, start : start + w].reshape(width, w)

        @pl.when(i == 0)
        def _():
            peers = [dev(lax.rem(z + d, NZ), y, xx, t) for d in range(1, NZ)] + plane
            hail(peers)

            @pl.loop(0, tokens // TB)
            def _(r):
                here = pl.ds(pl.multiple_of(r * TB, TB), TB)
                y_s[here, :] = ln_stats(x_ref[here, :].astype(F32))[0]

            hear(peers)
            begin()
            s_begin()
            for n in range(4):
                event(*order[n][1:])
            s_spread()
            for n in range(4, 7):
                event(*order[n][1:])
            done[0] = 7
            s_finish()

            @pl.loop(0, tokens // TB)
            def _(r):
                here = pl.ds(pl.multiple_of(r * TB, TB), TB)
                hn_s[here, :] = (y_s[here, :] * row(vecs, 0) + row(vecs, 1)).astype(BF)
                y_s[here, :] = jnp.zeros((TB, width), F32) + row(vecs, 2)

        for j in range(chunks):

            @pl.when(i == j)
            def _(j=j):
                until(j)

        @pl.when(i < chunks)
        def _():
            at = pl.multiple_of(i * HC, HC)
            odd = lax.rem(i, 2) == 1
            @pl.loop(0, 2)
            def _(t):
                w_in = ga[t, :, :, :, :, pl.ds(at, HC)].reshape(width, HC)
                w_out = ga[t, :, :, :, :, pl.ds(1024 + at, HC)].reshape(width, HC)
                line = vecs[pl.ds(R_B1 + 2 * t + i // 2, 1), :]
                bias = jnp.where(odd, line[:, HC:], line[:, :HC])
                for k in range(tokens // TB):
                    here = slice(k * TB, (k + 1) * TB)
                    zf = nn(hn_s[here, :], w_in) + bias
                    z_ref[here, pl.ds(pl.multiple_of(t * HC, HC), HC)] = zf.astype(BF)
                    y_s[here, :] += nt((zf * sig(zf)).astype(BF), w_out)

        @pl.when(i == chunks)
        def _():

            @pl.loop(0, tokens // TB)
            def _(r):
                here = pl.ds(pl.multiple_of(r * TB, TB), TB)
                first = x_ref[here, :].astype(F32) + 0.5 * y_s[here, :]
                y_s[here, :] = first
                scaled, _ = ln_stats(first)
                hn_s[here, :] = (scaled * row(vecs, 3) + row(vecs, 4)).astype(BF)
            copies[1].start()
            until(chunks)
            part = width // 2
            for t in range(2):
                c = slice(t * part, (t + 1) * part)
                pos[:, c] = nn(table_ref[...], weight(t, SEG["pos"][0], part)).astype(BF)
            copies[6].start()
            until(chunks + 1)
            copies[0].start()
            at = SEG["qkv"][0]
            @pl.loop(0, 2)
            def _(t):
                c = pl.ds(pl.multiple_of(t * part, part), part)

                lines = vecs[R_ATT:R_CV, :]
                lines = jnp.where(t == 0, lines[:, :part], lines[:, part:])

                @pl.loop(0, batch)
                def _(u):
                    hn = hn_s[pl.ds(pl.multiple_of(u * full, full), full), :]
                    q = nn(hn, weight(t, at, part)) + lines[0:1]
                    qu[u, :, c] = (q + lines[2:3]).astype(BF)
                    qv[u, :, c] = (q + lines[3:4]).astype(BF)
                    k[u, :, c] = nn(hn, weight(t, at + part, part)).astype(BF)
                    val = nn(hn, weight(t, at + 2 * part, part))
                    v[u, :, c] = (val + lines[1:2]).astype(BF)
            for n in (2, 3, 4, 5):
                copies[n].start()

        left = order[done[0] :]
        base = order[done[0] - 1][0] + 6.0
        blocks = full // BLK
        spots = batch * pairs * blocks
        slots = [min(max(int((now + 2.0 - base) / 0.9), 0), spots) for now, _, _ in left]

        def hook(blk):
            for slot, (_, kind, pair) in zip(slots, left):
                if slot % blocks == blk and slot < spots:

                    @pl.when(i == first_head + slot // blocks)
                    def _(kind=kind, pair=pair):
                        event(kind, pair)

        @pl.when(i >= first_head)
        def _():
            n = i - first_head
            u = n // pairs
            c = pl.ds(pl.multiple_of(lax.rem(n, pairs) * (2 * DK), 2 * DK), 2 * DK)

            def view(ref):
                return ref.at[pl.ds(u, 1), :, c]

            attn_fwd_kernel(
                len_ref, view(qu), view(qv), view(k), view(v), pos.at[:, c], view(mix), view(lse),
                u, hook,
            )

        @pl.when(i == steps - 1)
        def _():
            copies[7].start()
            copies[8].start()
            for slot, (_, kind, pair) in zip(slots, left):
                if slot >= spots:
                    event(kind, pair)
            finish()
            for copy in copies:
                copy.wait()

    def const(shape):
        return pl.BlockSpec(shape, lambda i, n: (0,) * len(shape), pipeline_mode=pl.Buffered(1))

    heads = jax.ShapeDtypeStruct(heads_shape, BF)
    return pl.pallas_call(
        body,
        grid_spec=pltpu.PrefetchScalarGridSpec(
            num_scalar_prefetch=1,
            grid=(steps,),
            in_specs=[
                const(x.shape), const(table.shape), const(packed_a.shape), const(packed_b.shape),
                const(packed_c.shape), const(slab.shape),
            ],
            out_specs=[
                ANY, ANY, ANY, pl.BlockSpec((R_ALL, width), lambda i, n: (0, 0)), ANY,
                pl.BlockSpec((tokens, 2 * HC), lambda i, n: (0, jnp.minimum(i, chunks - 1))),
            ]
            + [ANY] * 7,
            scratch_shapes=scratch + small + gather_scratch(len(FRONT_PIECES)),
        ),
        out_shape=[
            gathered_shape(packed_a),
            gathered_shape(packed_b),
            gathered_shape(packed_c),
            jax.ShapeDtypeStruct((R_ALL, width), F32),
            jax.ShapeDtypeStruct((tokens, width), F32),
            jax.ShapeDtypeStruct((tokens, 4 * width), BF),
            heads, heads, heads, heads,
            jax.ShapeDtypeStruct(table.shape, BF),
            heads,
            jax.ShapeDtypeStruct(heads_shape, F32),
        ],
        compiler_params=comm_params(cid),
        name="front",
    )(lens, x, table, packed_a, packed_b, packed_c, slab)


def fill_table(table_ref, first_s, second_s):
    length, width = table_ref.shape[0] // 2, table_ref.shape[1]
    step = 32
    cols = lax.broadcasted_iota(jnp.int32, (step, width), 1)
    rows = lax.broadcasted_iota(jnp.int32, (step, width), 0)
    rate = jnp.exp((cols // 2 * 2).astype(F32) * (-math.log(10000.0) / width))
    even = cols % 2 == 0
    big = (length - 1 - step * rows).astype(F32) * rate
    small = rows.astype(F32) * rate
    sin_big, cos_big = jnp.sin(big), jnp.cos(big)
    first = jnp.where(even, sin_big, cos_big)
    second = jnp.where(even, cos_big, -sin_big)
    cos_small, sin_small = jnp.cos(small), jnp.sin(small)
    first_s[...] = first
    second_s[...] = second

    @pl.loop(0, 2 * length // step)
    def _(a):
        one, two = first_s[pl.ds(a, 1), :], second_s[pl.ds(a, 1), :]
        block = one * cos_small - two * sin_small
        table_ref[pl.ds(pl.multiple_of(a * step, step), step), :] = block.astype(BF)


def table_call(full, width):
    return pl.pallas_call(
        fill_table,
        out_specs=VM,
        out_shape=jax.ShapeDtypeStruct((2 * full, width), BF),
        scratch_shapes=[pltpu.VMEM((32, width), F32)] * 2,
        name="position_table",
    )()


def conv1_kernel(
    lens, mixed, first, w_out, w_ci, vecs, second_ref, half_ref, conv_ref, stat_ref, pad
):
    u = pl.program_id(0)
    full = first.shape[0]
    count = lens[u]
    part = w_out.shape[2]
    y = row(vecs, 5)
    for t in range(2):
        y = y + nt(mixed[:, t * part : (t + 1) * part], w_out[t])
    second = first[...] + y
    second_ref[...] = second
    scaled, _ = ln_stats(second)
    hn = (scaled * row(vecs, 6) + row(vecs, 7)).astype(BF)
    mask = row_mask(0, full, count)
    pad[0:8, :] = jnp.zeros((8, part), F32)
    pad[full + 8 : full + 16, :] = jnp.zeros((8, part), F32)
    for t in range(2):
        c = slice(t * part, (t + 1) * part)
        proj = nn(hn, w_ci[t])
        za = proj[:, :part] + vecs[R_CV : R_CV + 1, c]
        zg = proj[:, part:] + vecs[R_CV + 1 : R_CV + 2, c]
        half_ref[:, 2 * t * part : (2 * t + 1) * part] = za.astype(BF)
        half_ref[:, (2 * t + 1) * part : (2 * t + 2) * part] = zg.astype(BF)
        pad[8 : full + 8, :] = za * sig(zg) * mask
        total = jnp.zeros((full, part), F32)
        for k in range(9):
            total = total + vecs[R_CV + 4 + k : R_CV + 5 + k, c] * pad[4 + k : 4 + k + full, :]
        conv_ref[:, c] = total
        kept = total * mask
        stat_ref[pl.ds(4 * u, 1), c] = col_sum(kept)
        stat_ref[pl.ds(4 * u + 1, 1), c] = col_sum(kept * total)
    for k in (2, 3):
        stat_ref[pl.ds(4 * u + k, 1), :] = jnp.full((1, 2 * part), 1.0, F32) * count.astype(F32)


def with_sum(kernel, spot, cid):
    def body(*refs):
        sums = refs[-8:]
        refs = list(refs[:-8])
        call, meet = sum_steps(sums)
        out = refs[spot]
        refs[spot] = sums[0]

        @pl.when(pl.program_id(0) == 0)
        def _():
            call()

        kernel(*refs)

        @pl.when(pl.program_id(0) == pl.num_programs(0) - 1)
        def _():
            for part in meet(out):
                part()

    return kernel if cid is None else body


def conv1_call(lens, mixed, first, g, vecs, cid=None):
    tokens, width = first.shape
    batch = lens.shape[0]
    full = tokens // batch
    return pl.pallas_call(
        with_sum(conv1_kernel, 9, cid),
        grid_spec=pltpu.PrefetchScalarGridSpec(
            num_scalar_prefetch=1,
            grid=(batch,),
            in_specs=[
                tall(full, width), tall(full, width), seg_spec("out", width),
                seg_spec("ci", width), whole(vecs.shape),
            ],
            out_specs=[
                tall(full, width), tall(full, 2 * width), tall(full, width),
                whole((4 * batch, width)),
            ],
            scratch_shapes=[pltpu.VMEM((full + 16, width // 2), F32)]
            + ([] if cid is None else sum_scratch((4 * batch, width))),
        ),
        out_shape=[
            jax.ShapeDtypeStruct((tokens, width), F32),
            jax.ShapeDtypeStruct((tokens, 2 * width), BF),
            jax.ShapeDtypeStruct((tokens, width), F32),
            jax.ShapeDtypeStruct((4 * batch, width), F32),
        ],
        compiler_params=dense_params() if cid is None else comm_params(cid),
        name="conv_forward",
    )(lens, mixed, first, g, g, vecs)


def bn_of(stats, u):
    n = stats[pl.ds(4 * u + 2, 1), :]
    avg = stats[pl.ds(4 * u, 1), :] / n
    var = stats[pl.ds(4 * u + 1, 1), :] / n - avg * avg
    return avg, lax.rsqrt(var + norm_eps), n


def swish_parts(z):
    s = sig(z)
    a = z * s
    return a, s + a * (1.0 - s)


def middle_kernel(
    lens, second, conv, cot, stats, w_co, w_in, w_out, vecs,
    act_ref, d3_ref, dy_ref, sum_ref, small_ref, gi_ref, go_ref, gc_ref,
    a_s, slope_s, gi, go, gc,
):
    i = pl.program_id(0)
    steps = pl.num_programs(0)
    rows, width = second.shape
    batch = lens.shape[0]
    per = steps // batch
    u = i // per
    mask = row_mask(lax.rem(i, per) * rows, rows, lens[u])

    @pl.when(i == 0)
    def _():
        small_ref[...] = jnp.zeros_like(small_ref)
        sum_ref[...] = jnp.zeros_like(sum_ref)
        gi[...] = jnp.zeros_like(gi)
        go[...] = jnp.zeros_like(go)
        gc[...] = jnp.zeros_like(gc)

    avg, rstd, _ = bn_of(stats, u)
    part = w_co.shape[2]
    half = w_in.shape[2]
    yhat = (conv[...] - avg) * rstd
    bn, bn_slope = swish_parts(yhat * row(vecs, R_CV + 2) + row(vecs, R_CV + 3))
    act = bn.astype(BF)
    y = row(vecs, 8)
    for t in range(2):
        y = y + nt(act[:, t * part : (t + 1) * part], w_co[t])
    third = second[...] + y
    scaled9, inv9 = ln_stats(third)
    hn = (scaled9 * row(vecs, 9) + row(vecs, 10)).astype(BF)
    y = row(vecs, 11)
    for t in range(2):
        c = slice(t * half, (t + 1) * half)
        a, slope = swish_parts(nn(hn, w_in[t]) + bias_half(vecs, R_B2, t))
        a = a.astype(BF)
        a_s[:, c] = a
        slope_s[:, c] = slope
        y = y + nt(a, w_out[t])
    scaled, inv = ln_stats(third + 0.5 * y)
    act_ref[...] = (scaled * row(vecs, 12) + row(vecs, 13)).astype(BF)
    up = cot[...].astype(F32) * mask
    small_ref[12:13, :] += col_sum(up * scaled)
    small_ref[13:14, :] += col_sum(up)
    d4 = ln_back(up, scaled, inv, row(vecs, 12))
    g = (0.5 * d4).astype(BF)
    small_ref[11:12, :] += col_sum(g.astype(F32))
    d_hn = jnp.zeros((rows, width), F32)
    for t in range(2):
        c = slice(t * half, (t + 1) * half)
        go[t] += tn(g, a_s[:, c])
        dz = (nn(g, w_out[t]) * slope_s[:, c]).astype(BF)
        bias = col_sum(dz.astype(F32))
        small_ref[R_B2 + 2 * t : R_B2 + 2 * t + 1, :] += bias[:, :width]
        small_ref[R_B2 + 2 * t + 1 : R_B2 + 2 * t + 2, :] += bias[:, width:]
        gi[t] += tn(hn, dz)
        d_hn = d_hn + nt(dz, w_in[t])
    small_ref[9:10, :] += col_sum(d_hn * scaled9)
    small_ref[10:11, :] += col_sum(d_hn)
    d3 = d4 + ln_back(d_hn, scaled9, inv9, row(vecs, 9))
    d3_ref[...] = d3
    g = d3.astype(BF)
    small_ref[8:9, :] += col_sum(g.astype(F32))
    d_act = []
    for t in range(2):
        gc[t] += tn(g, act[:, t * part : (t + 1) * part])
        d_act.append(nn(g, w_co[t]))
    d_bn = jnp.concatenate(d_act, axis=1) * bn_slope
    small_ref[R_CV + 2 : R_CV + 3, :] += col_sum(d_bn * yhat)
    small_ref[R_CV + 3 : R_CV + 4, :] += col_sum(d_bn)
    d_yhat = d_bn * row(vecs, R_CV + 2)
    dy_ref[...] = d_yhat
    sum_ref[pl.ds(4 * u, 1), :] += col_sum(d_yhat)
    sum_ref[pl.ds(4 * u + 1, 1), :] += col_sum(d_yhat * yhat)

    @pl.when(i == steps - 1)
    def _():
        gi_ref[...] = gi[...].astype(BF)
        go_ref[...] = go[...].astype(BF)
        gc_ref[...] = gc[...].astype(BF)


def grad_shape(name, width):
    return jax.ShapeDtypeStruct((2, width, SEG[name][1]), BF)


def acc(name, width):
    return pltpu.VMEM((2, width, SEG[name][1]), F32)


def once(shape):
    zeros = (0,) * len(shape)
    return pl.BlockSpec(shape, lambda i, *_: zeros, pipeline_mode=pl.Buffered(1))


def middle_call(lens, second, conv, cot, stats, g, g_f2, vecs, cid=None):
    tokens, width = second.shape
    small = (R_ALL, width)
    names = ("f2i", "f2o", "co")
    return pl.pallas_call(
        with_sum(middle_kernel, 12, cid),
        grid_spec=pltpu.PrefetchScalarGridSpec(
            num_scalar_prefetch=1,
            grid=(tokens // TB,),
            in_specs=[tall(TB, width)] * 3
            + [whole(stats.shape), seg_spec("co", width), seg_spec("f2i", width)]
            + [seg_spec("f2o", width), whole(vecs.shape)],
            out_specs=[tall(TB, width)] * 3
            + [whole(stats.shape), whole(small)]
            + [whole(grad_shape(name, width).shape) for name in names],
            scratch_shapes=[
                pltpu.VMEM((TB, 4 * width), BF),
                pltpu.VMEM((TB, 4 * width), F32),
            ]
            + [acc(name, width) for name in names]
            + ([] if cid is None else sum_scratch(stats.shape)),
        ),
        out_shape=[
            jax.ShapeDtypeStruct((tokens, width), BF),
            jax.ShapeDtypeStruct((tokens, width), F32),
            jax.ShapeDtypeStruct((tokens, width), F32),
            jax.ShapeDtypeStruct(stats.shape, F32),
            jax.ShapeDtypeStruct(small, F32),
        ]
        + [grad_shape(name, width) for name in names],
        compiler_params=dense_params() if cid is None else comm_params(cid),
        name="conv_out_ffn2",
    )(lens, second, conv, cot, stats, g, g_f2, g_f2, vecs)


def conv2_kernel(
    lens, dy, conv, d3, halves, second, mixed, stats, sums, w_ci, w_out, vecs,
    d2_ref, dm_ref, small_ref, gi_ref, go_ref, pad, dh_s, gi, go,
):
    u = pl.program_id(0)
    full, width = d3.shape
    part = w_out.shape[2]

    @pl.when(u == 0)
    def _():
        small_ref[...] = jnp.zeros_like(small_ref)
        gi[...] = jnp.zeros_like(gi)
        go[...] = jnp.zeros_like(go)

    avg, rstd, n = bn_of(stats, u)
    mask = row_mask(0, full, lens[u])
    scaled, inv = ln_stats(second[...])
    hn = (scaled * row(vecs, 6) + row(vecs, 7)).astype(BF)
    pad[0:8, :] = jnp.zeros((8, part), F32)
    pad[full + 8 : full + 16, :] = jnp.zeros((8, part), F32)
    b1 = sums[pl.ds(4 * u, 1), :]
    b2 = sums[pl.ds(4 * u + 1, 1), :]
    dh_s[...] = jnp.zeros_like(dh_s)
    taps = vecs[R_CV : R_CV + 13, :]

    @pl.loop(0, 2)
    def _(t):
        c = pl.ds(pl.multiple_of(t * part, part), part)

        def lanes(v):
            return jnp.where(t == 0, v[:, :part], v[:, part:])

        yhat = (conv[:, c] - lanes(avg)) * lanes(rstd)
        pad[8 : full + 8, :] = lanes(rstd) * (
            dy[:, c] - mask * ((lanes(b1) + yhat * lanes(b2)) / lanes(n))
        )
        za = halves[:, pl.ds(pl.multiple_of(2 * t * part, part), part)].astype(F32)
        zg = halves[:, pl.ds(pl.multiple_of((2 * t + 1) * part, part), part)].astype(F32)
        gate = sig(zg)
        gated = za * gate * mask
        total = jnp.zeros((full, part), F32)
        mine = lanes(taps)
        for k in range(9):
            moved = pad[12 - k : 12 - k + full, :]
            total = total + mine[4 + k : 5 + k, :] * moved
            small_ref[R_CV + 4 + k : R_CV + 5 + k, c] += col_sum(gated * moved)
        d_glu = total * mask
        d_a = (d_glu * gate).astype(BF)
        d_g = (d_glu * gated * (1.0 - gate)).astype(BF)
        small_ref[R_CV : R_CV + 1, c] += col_sum(d_a.astype(F32))
        small_ref[R_CV + 1 : R_CV + 2, c] += col_sum(d_g.astype(F32))
        pair = jnp.concatenate([d_a, d_g], axis=1)
        gi[t] += tn(hn, pair)
        dh_s[...] += nt(pair, w_ci[t])

    d_hn = dh_s[...]
    small_ref[6:7, :] += col_sum(d_hn * scaled)
    small_ref[7:8, :] += col_sum(d_hn)
    d2 = d3[...] + ln_back(d_hn, scaled, inv, row(vecs, 6))
    d2_ref[...] = d2
    g = d2.astype(BF)
    small_ref[5:6, :] += col_sum(g.astype(F32))
    @pl.loop(0, 2)
    def _(t):
        c = pl.ds(pl.multiple_of(t * part, part), part)
        go[t] += tn(g, mixed[:, c])
        dm_ref[:, c] = nn(g, w_out[t]).astype(BF)

    @pl.when(u == pl.num_programs(0) - 1)
    def _():
        gi_ref[...] = gi[...].astype(BF)
        go_ref[...] = go[...].astype(BF)


def conv2_call(lens, dy, conv, d3, halves, second, mixed, stats, sums, g, vecs):
    tokens, width = second.shape
    batch = lens.shape[0]
    full = tokens // batch
    small = (R_ALL, width)
    names = ("ci", "out")
    return pl.pallas_call(
        conv2_kernel,
        grid_spec=pltpu.PrefetchScalarGridSpec(
            num_scalar_prefetch=1,
            grid=(batch,),
            in_specs=[tall(full, width)] * 3
            + [tall(full, 2 * width), tall(full, width), tall(full, width)]
            + [whole(stats.shape)] * 2
            + [seg_spec("ci", width), seg_spec("out", width), whole(vecs.shape)],
            out_specs=[tall(full, width)] * 2
            + [whole(small)]
            + [whole(grad_shape(name, width).shape) for name in names],
            scratch_shapes=[
                pltpu.VMEM((full + 16, width // 2), F32), pltpu.VMEM((full, width), F32),
            ]
            + [acc(name, width) for name in names],
        ),
        out_shape=[
            jax.ShapeDtypeStruct((tokens, width), F32),
            jax.ShapeDtypeStruct((tokens, width), BF),
            jax.ShapeDtypeStruct(small, F32),
        ]
        + [grad_shape(name, width) for name in names],
        compiler_params=dense_params(),
        name="conv_backward",
    )(lens, dy, conv, d3, halves, second, mixed, stats, sums, g, g, vecs)


def last_kernel(
    dq, dk, dv, first, x_ref, d2, z_ref, table, dpos, asums, w_qkv, w_in, w_out, vecs,
    d0_ref, small_ref, d1_s, g_s, hn_s, dh_s, gq, gp, z_s, w_in_s, w_out_s, in_sem,
    put, ready, after,
):
    i = pl.program_id(0)
    blocks = x_ref.shape[0] // TB
    rows, width = first.shape
    part = w_qkv.shape[2] // 3
    ahead = [
        pltpu.make_async_copy(w_in.at[:, :, pl.ds(0, w_in_s.shape[2])], w_in_s, in_sem.at[0]),
        pltpu.make_async_copy(
            w_out.at[:, :, pl.ds(w_in_s.shape[2], w_in_s.shape[2])], w_out_s, in_sem.at[1]
        ),
        pltpu.make_async_copy(z_ref, z_s, in_sem.at[2]),
    ]

    @pl.when(i == 0)
    def _():
        small_ref[...] = jnp.zeros_like(small_ref)
        small_ref[R_ATT:R_CV, :] = jnp.sum(asums[...], axis=0)[0:4]
        for copy in ahead:
            copy.start()
        gq[...] = jnp.zeros_like(gq)
        gp[...] = jnp.zeros_like(gp)
        dh_s[...] = jnp.zeros_like(dh_s)

    @pl.when(i < blocks)
    def _():
        here = pl.ds(pl.multiple_of(i * TB, TB), TB)
        scaled, inv = ln_stats(first[...])
        hn = (scaled * row(vecs, 3) + row(vecs, 4)).astype(BF)
        d_hn = jnp.zeros((rows, width), F32)
        for t in range(2):
            c = slice(t * part, (t + 1) * part)
            dp = jnp.concatenate([dq[:, c], dk[:, c], dv[:, c]], axis=1)
            gq[t] += tn(hn, dp)
            for u in range(dpos.shape[0]):
                gp[t] += tn(table[...], dpos[u, :, c])
            d_hn = d_hn + nt(dp, w_qkv[t])
        small_ref[3:4, :] += col_sum(d_hn * scaled)
        small_ref[4:5, :] += col_sum(d_hn)
        d1 = d2[...] + ln_back(d_hn, scaled, inv, row(vecs, 3))
        d1_s[here, :] = d1
        g = (0.5 * d1).astype(BF)
        g_s[here, :] = g
        small_ref[2:3, :] += col_sum(g.astype(F32))
        scaled, inv = ln_stats(x_ref[here, :].astype(F32))
        hn_s[here, :] = (scaled * row(vecs, 0) + row(vecs, 1)).astype(BF)

    @pl.when(i == blocks - 1)
    def _():
        for t in range(2):
            put("pos", t, 0, gp[t])
            put("qkv", t, 0, gq[t])
        for copy in ahead:
            copy.wait()
        ready(-1)

    chunks = w_in_s.shape[2] // HC

    @pl.when(i >= blocks)
    def _():
        j = i - blocks
        at = pl.multiple_of(j * HC, HC)
        c = pl.ds(at, HC)
        odd = lax.rem(j, 2) == 1
        @pl.loop(0, 2)
        def _(t):
            zc = pl.ds(pl.multiple_of((2 * j + t) * HC, HC), HC)
            a, slope = swish_parts(z_s[:, zc].astype(F32))
            put("f1o", t, at, tn(g_s[...], a.astype(BF)))
            dz = (nn(g_s[...], w_out_s[t, :, c]) * slope).astype(BF)
            bias = col_sum(dz.astype(F32))
            none = jnp.zeros_like(bias)
            pair = [jnp.where(odd, none, bias), jnp.where(odd, bias, none)]
            line = pl.ds(R_B1 + 2 * t + j // 2, 1)
            small_ref[line, :] += jnp.concatenate(pair, axis=1)
            put("f1i", t, at, tn(hn_s[...], dz))
            dh_s[...] += nt(dz, w_in_s[t, :, c])
            for k in range(chunks):
                for side in range(2):

                    @pl.when((j == k) & (t == side))
                    def _(k=k, side=side):
                        after(k, side)

        for k in range(chunks):

            @pl.when(j == k)
            def _(k=k):
                ready(k)

    @pl.when(i == blocks + chunks - 1)
    def _():
        @pl.loop(0, blocks)
        def _(k):
            here = pl.ds(pl.multiple_of(k * TB, TB), TB)
            scaled, inv = ln_stats(x_ref[here, :].astype(F32))
            d_hn = dh_s[here, :]
            small_ref[0:1, :] += col_sum(d_hn * scaled)
            small_ref[1:2, :] += col_sum(d_hn)
            d0 = d1_s[here, :] + ln_back(d_hn, scaled, inv, row(vecs, 0))
            d0_ref[here, :] = d0.astype(BF)


def last_call(dq, dk, dv, first, x, d2, z, table, dpos, asums, g, vecs, others=None, cid=None):
    tokens, width = first.shape
    blocks, chunks = tokens // TB, SEG["f1i"][1] // HC
    small = (R_ALL, width)
    places = table.shape[0] // blocks

    def block(rows, cols):
        return pl.BlockSpec((rows, cols), lambda i: (jnp.minimum(i, blocks - 1), 0))

    in_specs = (
        [block(TB, width)] * 4
        + [whole(x.shape), block(TB, width)]
        + [ANY]
        + [block(places, width)]
        + [
            pl.BlockSpec(
                (dpos.shape[0], places, width), lambda i: (0, jnp.minimum(i, blocks - 1), 0)
            ),
            whole(asums.shape),
        ]
        + [seg_spec("qkv", width), ANY, ANY, whole(vecs.shape)]
    )
    args = [dq, dk, dv, first, x, d2, z, table, dpos, asums, g, g, g, vecs]
    scratch = [
        pltpu.VMEM((tokens, width), F32), pltpu.VMEM((tokens, width), BF),
        pltpu.VMEM((tokens, width), BF), pltpu.VMEM((tokens, width), F32),
        acc("qkv", width), acc("pos", width), pltpu.VMEM(z.shape, BF),
        pltpu.VMEM((2, width, SEG["f1i"][1]), BF), pltpu.VMEM((2, width, SEG["f1o"][1]), BF),
        pltpu.SemaphoreType.DMA((3,)),
    ]
    out_specs = [whole((tokens, width)), whole(small)]
    out_shape = [jax.ShapeDtypeStruct((tokens, width), BF), jax.ShapeDtypeStruct(small, F32)]
    n_own = len(scratch)
    if others is None:
        names = ("qkv", "f1i", "f1o", "pos")
        out_specs += [once(grad_shape(name, width).shape) for name in names]
        out_shape += [grad_shape(name, width) for name in names]

        def body(*refs):
            ins, rest = refs[: len(args)], refs[len(args) :]
            outs = dict(zip(names, rest[2:6]))

            def put(name, t, at, value):
                outs[name][t, :, pl.ds(at, value.shape[1])] = value.astype(BF)

            last_kernel(*ins, *rest[:2], *rest[6:], put, lambda j: None, lambda j, t: None)

        params = dense_params()
    else:
        owned = width // (NZ * NY * NX)
        names = ("pos", "qkv", "f1i", "f1o")
        base = {name: SEG[name][0] for name in names}
        order = [("pos", 0), ("qkv", 0), ("qkv", 256), ("qkv", 512)]
        for j in range(chunks):
            order += [("f1i", j * HC), ("f1o", j * HC)]
        pieces = [(0, base[name] + at, 256, base[name] + at) for name, at in order]
        n_first = 4
        n_in = len(args)
        args += list(others)
        in_specs += [whole(item.shape) for item in others]
        out_specs = out_specs[:1] + [whole((owned, C_A)), whole((R_SUM, width))]
        out_shape = out_shape[:1] + [
            jax.ShapeDtypeStruct((owned, C_A), F32), jax.ShapeDtypeStruct((R_SUM, width), F32)
        ]
        small_scratch = small_sum_scratch(width)
        scratch += [pltpu.VMEM(small, F32), pltpu.VMEM((2, NZ, NY, NX, owned, C_A), BF)]
        scratch += small_scratch + scatter_scratch(pieces, owned)
        params = comm_params(cid)

        def body(*refs):
            i = pl.program_id(0)
            ins, rest = refs[:n_in], refs[n_in:]
            parts, rest = rest[: len(others)], rest[len(others) :]
            (d0_ref, o_ref, ext), rest = rest[:3], rest[3:]
            own, rest = rest[:n_own], rest[n_own:]
            (small_ref, buf), rest = rest[:2], rest[2:]
            sums, sems = rest[: len(small_scratch)], rest[len(small_scratch) :]
            start, advance, finish, rounds = scatter_steps(pieces, [buf], o_ref, sems, 4)
            pp, small_list = small_sum_steps(list(parts) + [small_ref], ext, sums)
            z, y, x, t = place()

            def put(name, t, at, value):
                w = value.shape[1]
                at = base[name] + at
                at = at if isinstance(at, int) else pl.multiple_of(at, HC)
                value = value.astype(BF).reshape(NZ, NY, NX, owned, w)
                buf[t, :, :, :, :, pl.ds(at, w)] = value

            def ready(j):
                if j < 0:
                    hear(peers)
                for p in range(n_first) if j < 0 else (n_first + 2 * j, n_first + 2 * j + 1):
                    start(p)

            def after(j, t):
                if j == 0:
                    advance(2 * t)
                    advance(2 * t + 1)
                else:
                    advance(n_first + 2 * (j - 1) + t)

            peers = link_peers(z, y, x, t)[: NZ - 1] + pp + [dev(z, y, x, 1 - t)]

            @pl.when(i == 0)
            def _():
                hail(peers)

            last_kernel(*ins, d0_ref, small_ref, *own, put, ready, after)

            @pl.when(i == blocks + chunks - 1)
            def _():
                todo = [lambda q=q: advance(q) for q in range(n_first + 2 * (chunks - 1), rounds)]
                for k, step in enumerate(todo):
                    if k % 2 == 0 and k // 2 < len(small_list):
                        small_list[k // 2]()
                    step()
                for step in small_list[(len(todo) + 1) // 2 :]:
                    step()
                finish()

    return pl.pallas_call(
        body,
        grid=(blocks + chunks,),
        in_specs=in_specs,
        out_specs=out_specs,
        scratch_shapes=scratch,
        out_shape=out_shape,
        compiler_params=params,
        name="qkv_ffn1_backward",
    )(*args)


def gather_plain(big, kinds, groups, small_ins, both, n_dp):
    def pack(names):
        return jnp.concatenate(
            [big[n].T if kinds[n][0] == "flip" else big[n] for n in names], axis=1
        )

    def every(item):
        g = lax.all_gather(item, both, axis=0, tiled=True)
        g = g.reshape(n_dp, 2, item.shape[0], -1).transpose(1, 0, 2, 3)
        return g.reshape(2, n_dp * item.shape[0], -1)

    small = jnp.concatenate([item.reshape(-1) for item in small_ins])
    smalls = lax.all_gather(small, both, axis=0, tiled=False).reshape(n_dp, 2, -1).astype(F32)
    off = 0
    pieces = []
    for item in small_ins:
        pieces.append(smalls[:, :, off : off + item.size].reshape((n_dp, 2) + item.shape))
        off += item.size
    width = small_ins[4].shape[1] * n_dp * 2
    vecs = jnp.concatenate(
        [
            pieces[4].transpose(2, 0, 1, 3).reshape(-1, width),
            pieces[1].transpose(2, 1, 3, 0, 4).reshape(-1, width),
            pieces[2].transpose(2, 1, 3, 0, 4).reshape(-1, width),
            pieces[0].transpose(1, 2, 0, 3).reshape(-1, width),
            pieces[3].transpose(1, 2, 0, 3).reshape(-1, width),
            jnp.zeros((1, width), F32),
        ],
        axis=0,
    )
    return tuple(every(pack(names)) for names in groups) + (vecs,)


def scatter_plain(grads, kinds, names, small_g, small_ins, both, n_dp):
    vec_g = (
        small_g[R_B1:R_B2].reshape(1, -1), small_g[R_ATT:R_CV], small_g[R_CV:R_B1],
        small_g[R_B2 : R_B2 + 4].reshape(1, -1),
    )

    def small_of(item, like):
        item = item.reshape(item.shape[0], 2, like.shape[-2], n_dp, like.shape[-1])
        return item.transpose(1, 3, 0, 2, 4).reshape(2, n_dp, -1)

    cols = small_ins[4].shape[1]
    norm_g = small_g[:R_ATT].reshape(-1, n_dp, 2, cols).transpose(2, 1, 0, 3).reshape(2, n_dp, -1)
    packed = jnp.concatenate(
        [small_of(item, like) for item, like in zip(vec_g, small_ins)] + [norm_g], axis=2
    )
    packed = packed.swapaxes(0, 1).reshape(n_dp * 2, -1)
    own_small = lax.psum_scatter(packed, both, scatter_dimension=0, tiled=True).reshape(-1)
    wide = jnp.concatenate([grads[name] for name in names], axis=2)
    rows = wide.shape[1] // n_dp
    wide = wide.reshape(2, n_dp, rows, -1).swapaxes(0, 1).reshape(n_dp * 2 * rows, -1)
    own = lax.psum_scatter(wide, both, scatter_dimension=0, tiled=True).astype(F32)
    outs, at = {}, 0
    for name in names:
        w = grads[name].shape[2]
        item = own[:, at : at + w]
        outs[name] = item.T if kinds[name][0] == "flip" else item
        at += w
    small_outs, at = [], 0
    for item in small_ins:
        small_outs.append(own_small[at : at + item.size].reshape(item.shape))
        at += item.size
    return outs, small_outs


def local(
    frames,
    lengths,
    ffn1_in,
    ffn1_out,
    ffn1_bias,
    qkv_weight,
    pos_weight,
    out_weight,
    attn_bias,
    conv_in,
    conv_out,
    conv_channel,
    ffn2_in,
    ffn2_out,
    ffn2_bias,
    norm_params,
    cotangent,
):
    micro, seqs, full, width = frames.shape
    both = ("dp", "tensor")
    n_dp = lax.axis_size("dp")
    rows = ffn1_in.shape[0]
    batch = micro * seqs
    tokens = batch * full
    small_ins = (ffn1_bias, attn_bias, conv_channel, ffn2_bias, norm_params)
    names_a, names_b = ("f1i", "f1o", "pos", "qkv"), tuple(OWN)
    big = {
        "f1i": ffn1_in, "f1o": ffn1_out, "pos": pos_weight, "qkv": qkv_weight.reshape(rows, -1),
        "f2i": ffn2_in, "f2o": ffn2_out, "ci": conv_in.reshape(rows, -1), "out": out_weight,
        "co": conv_out,
    }
    kinds = {name: ("plain",) for name in big}
    kinds.update({name: ("flip",) for name in ("f1o", "f2o", "out", "co")})
    mine_mesh = own_mesh((n_dp, lax.axis_size("tensor"))) and rows % 16 == 0
    if mine_mesh:
        packed_a, packed_b, packed_c, slab, table = prep_call(
            [
                ffn1_in, ffn1_out.T, pos_weight, qkv_weight.transpose(1, 0, 2), ffn2_in,
                ffn2_out.T, conv_in, out_weight.T, conv_out.T,
            ],
            [ffn1_bias, attn_bias, conv_channel.transpose(1, 2, 0), ffn2_bias, norm_params],
            full, width,
        )
    else:
        table = table_call(full, width)
        groups = (names_a, names_b[2:], names_b[:2])
        g_a, g_b, g_c, vecs = gather_plain(big, kinds, groups, small_ins, both, n_dp)

    def reduce_sum(item):
        return item if mine_mesh else lax.psum(item, both)

    mine = lax.axis_index("tensor")
    lens = lax.dynamic_slice_in_dim(lengths, mine * seqs, seqs, 1).reshape(-1)
    x = frames.reshape(tokens, width)
    cot = cotangent.reshape(tokens, width)

    def utt(item):
        return item.reshape(batch, full, -1)

    def flat(item):
        return item.reshape(tokens, -1)

    if mine_mesh:
        g_a, g_b, g_c, vecs, first, z1, q_u, q_v, keys, values, pos, mixed, lse = front_call(
            lens, x, table, packed_a, packed_b, packed_c, slab, batch, 1
        )
        g_a, g_b, g_c = (item.reshape(2, width, -1) for item in (g_a, g_b, g_c))
        heads = (lens, q_u, q_v, keys, values, pos)
    else:
        first, z1, q_u, q_v, keys, values, pos = ffn1_call(x, table, g_a, vecs)
        heads = (lens, utt(q_u), utt(q_v), utt(keys), utt(values), pos)
        mixed, lse = attn_fwd_call(*heads)
    second, halves, conv, stats = conv1_call(
        lens, flat(mixed), first, g_b, vecs, 3 if mine_mesh else None
    )
    stats = reduce_sum(stats)
    grads = {}
    result, d3, d_yhat, sums, small_m, grads["f2i"], grads["f2o"], grads["co"] = middle_call(
        lens, second, conv, cot, stats, g_b, g_c, vecs, 4 if mine_mesh else None
    )
    sums = reduce_sum(sums)
    d2, d_mixed, small_c, grads["ci"], grads["out"] = conv2_call(
        lens, d_yhat, conv, d3, halves, second, flat(mixed), stats, sums, g_b, vecs
    )
    if mine_mesh:
        dq, dk, dv, dpos, asums, own_b = attn_bwd_call(
            *heads, mixed, lse, utt(d_mixed), [grads[name] for name in names_b], 5
        )
        d0, own_a, ext = last_call(
            flat(dq), flat(dk), flat(dv), first, x, d2, z1, table, dpos, asums, g_a, vecs,
            (small_m, small_c), 6,
        )
        outs = finish_call(own_a, own_b, ext, rows)
    else:
        dq, dk, dv, dpos, asums = attn_bwd_call(*heads, mixed, lse, utt(d_mixed))
        d0, small_l, grads["qkv"], grads["f1i"], grads["f1o"], grads["pos"] = last_call(
            flat(dq), flat(dk), flat(dv), first, x, d2, z1, table, dpos, asums, g_a, vecs
        )
        o, small_outs = scatter_plain(
            grads, kinds, names_a + names_b, small_m + small_c + small_l, small_ins, both, n_dp
        )
        outs = (
            o["f1i"], o["f1o"], small_outs[0], o["qkv"].reshape(qkv_weight.shape), o["pos"],
            o["out"], small_outs[1], o["ci"].reshape(conv_in.shape), o["co"], small_outs[2],
            o["f2i"], o["f2o"], small_outs[3], small_outs[4],
        )
    return (result.reshape(frames.shape), d0.reshape(frames.shape)) + tuple(outs)


def solution(mesh):
    in_specs = (
        P(None, ("dp", "tensor"), None, None),
        P(None, "dp"),
        P("dp", "tensor"),
        P("tensor", "dp"),
        P("tensor", "dp"),
        P("dp", None, "tensor"),
        P("dp", "tensor"),
        P("tensor", "dp"),
        P(None, "tensor", "dp"),
        P("dp", None, "tensor"),
        P("tensor", "dp"),
        P(None, "tensor", "dp"),
        P("dp", "tensor"),
        P("tensor", "dp"),
        P("tensor", "dp"),
        P(None, ("dp", "tensor")),
        P(None, ("dp", "tensor"), None, None),
    )
    out_specs = (
        P(None, ("dp", "tensor"), None, None),
        P(None, ("dp", "tensor"), None, None),
        P("dp", "tensor"),
        P("tensor", "dp"),
        P("tensor", "dp"),
        P("dp", None, "tensor"),
        P("dp", "tensor"),
        P("tensor", "dp"),
        P(None, "tensor", "dp"),
        P("dp", None, "tensor"),
        P("tensor", "dp"),
        P(None, "tensor", "dp"),
        P("dp", "tensor"),
        P("tensor", "dp"),
        P("tensor", "dp"),
        P(None, ("dp", "tensor")),
    )
    return jax.shard_map(local, mesh=mesh, in_specs=in_specs, out_specs=out_specs, check_vma=False)
```

profile of v0, /device:TPU:0, one launch (start us, length us, event | category | flops | bytes accessed | tf_op | source)
XLA Modules:
  0.0 298.9 jit_solution(1392505340524674368)
XLA Ops:
  0.6 0.0 copy-start
  0.7 0.7 copy-done
  1.3 0.7 dynamic-slice_reduce_fusion.len_ref.refs_0_.lens
  2.0 3.2 %prepare.1 = (bf16[32,3072]{1,0:T(8,128)(2,1)}, bf16[32,1024]{1,0:T(8,128)(2,1)}, bf16[32,2048]{1,0:T(8,128)(2,1)}, bf16[112,128]{1,0:T(8,128)(2,1)}, bf16[1024,512]{1,0:T(8,128)(2,1)}) custom-call(bf16[32,1024]{1,0:T(8,128)(2,1)} %f1i.1, bf16[32,1024]{1,0:T(8,128)(2,1)} %bitcast.59, bf16[32,256]{1,0:T(8,128)(2,1)} %pos.1, bf16[3,32,256]{2,1,0:T(8,128)(2,1)} %bitcast.61, ...), custom_call_target="tpu_custom_call" | custom-call | tf_op jit(solution)/shard_map/prepare/pallas_call | solution.py:532
  5.2 91.0 %front.1 = (bf16[2,4,2,2,32,3072]{5,4,3,2,1,0:T(8,128)(2,1)}, bf16[2,4,2,2,32,1024]{5,4,3,2,1,0:T(8,128)(2,1)}, bf16[2,4,2,2,32,2048]{5,4,3,2,1,0:T(8,128)(2,1)}...) custom-call(s32[2]{0:T(128)} %dynamic-slice_reduce_fusion.len_ref.re, ...), custom_call_target="tpu_custom_call" | custom-call | tf_op jit(solution)/shard_map/front/pallas_call | solution.py:1104
  96.2 19.6 %conv_forward.1 = (f32[1024,512]{1,0:T(8,128)}, bf16[1024,1024]{1,0:T(8,128)(2,1)}, f32[1024,512]{1,0:T(8,128)}, f32[8,512]{1,0:T(8,128)}) custom-call(s32[2]{0:T(128)} %dynamic-slice_reduce_fusion.len_ref.refs_0_.lens, bf16[1024,512]{1,0:T(8,128)(2,1)} %bitcast.43, f32[1024,512]{1,0:T(8,128)} %get-tuple-element.80.refs_2_.refs_3_, ...), custom_call_target="tpu_custom_call" | custom-call | tf_op jit(solution)/shard_map/conv_forward/pallas_call | solution.py:1232
  115.8 36.4 %conv_out_ffn2.1 = (bf16[1024,512]{1,0:T(8,128)(2,1)}, f32[1024,512]{1,0:T(8,128)}, f32[1024,512]{1,0:T(8,128)}, f32[8,512]{1,0:T(8,128)}, f32[40,512]{1,0:T(8,1...) custom-call(s32[2]{0:T(128)} %dynamic-slice_reduce_fusion.len_ref.refs_0_.lens, ...), custom_call_target="tpu_custom_call" | custom-call | tf_op jit(solution)/shard_map/conv_out_ffn2/pallas_call | solution.py:1373
  152.2 21.2 %conv_backward.1 = (f32[1024,512]{1,0:T(8,128)}, bf16[1024,512]{1,0:T(8,128)(2,1)}, f32[40,512]{1,0:T(8,128)}, bf16[2,512,512]{2,1,0:T(8,128)(2,1)}, bf16[2,512,256]{2,1,0:T(8,128)(2,1)}) custom-call(s32[2]{0:T(128)} %dynamic-slice_reduce_fusion.len_ref.refs_0_.lens, f32[1024,512]{1,0:T(8,128)} %get-tuple-element.94.dy, ...), custom_call_target="tpu_custom_call" | custom-call | tf_op jit(solution)/shard_map/conv_backward/pallas_call | solution.py:1484
  173.4 68.7 %attn_bwd.1 = (bf16[2,512,512]{2,1,0:T(8,128)(2,1)}, bf16[2,512,512]{2,1,0:T(8,128)(2,1)}, bf16[2,512,512]{2,1,0:T(8,128)(2,1)}, bf16[2,1024,512]{2,1,0:T(8,128)...) custom-call(s32[2]{0:T(128)} %dynamic-slice_reduce_fusion.len_ref.refs_0_.lens, ...), custom_call_target="tpu_custom_call" | custom-call | tf_op jit(solution)/shard_map/attn_bwd/pallas_call | solution.py:217
  242.1 0.0 copy-start.1
  242.2 52.3 %qkv_ffn1_backward.1 = (bf16[1024,512]{1,0:T(8,128)(2,1)}, f32[32,3072]{1,0:T(8,128)}, f32[48,512]{1,0:T(8,128)}) custom-call(bf16[1024,512]{1,0:T(8,128)(2,1)} %bitcast.52, bf16[1024,512]{1,0:T(8,128)(2,1)} %bitcast.53, bf16[1024,512]{1,0:T(8,128)(2,1)} %bitcast.54, f32[1024,512]{1,0:T(8,128)} %get-tuple-element.80.refs_2_.refs_3_, ...), custom_call_target="tpu_custom_call" | custom-call | tf_op jit(solution)/shard_map/qkv_ffn1_backward/pallas_call | solution.py:1738
  294.4 0.0 copy-start.2
  294.5 2.5 own_gradients.1
  297.0 0.0 copy-done.1
  297.0 1.0 copy.37
  298.0 0.0 copy-done.2
  298.0 1.0 copy.38
Async XLA Ops:
  0.6 0.7 copy-start
  242.1 54.8 %copy-start.1 = (bf16[1024,512]{1,0:T(8,128)(2,1)S(1)}, bf16[1024,512]{1,0:T(8,128)(2,1)}, u32[]{:S(2)}) copy-start(bf16[1024,512]{1,0:T(8,128)(2,1)} %get-tuple-element.87) | copy-start | bytes 3145732
  294.4 3.5 %copy-start.2 = (bf16[1024,512]{1,0:T(8,128)(2,1)S(1)}, bf16[1024,512]{1,0:T(8,128)(2,1)}, u32[]{:S(2)}) copy-start(bf16[1024,512]{1,0:T(8,128)(2,1)} %get-tuple-element.114) | copy-start | bytes 3145732
where the time goes:
time: 299 us
  Pallas kernels  295 us (99%)
  local copies, waits for them, and re-layouts  3.32 us (1%)
    pallas_call x1, Pallas kernels, front_call(): pl.pallas_call(body, grid_spec=pltpu.PrefetchScalarGridSpec(num_scalar_pr...  91 us
    pallas_call x1, Pallas kernels, attn_bwd_call(): pl.pallas_call(body, grid_spec=pltpu.PrefetchScalarGridSpec(num_scalar_pr...  68.7 us
    pallas_call x1, Pallas kernels, last_call(): pl.pallas_call(body, grid=(blocks + chunks,), in_specs=in_specs, out_spec...  52.3 us
    pallas_call x1, Pallas kernels, middle_call(): pl.pallas_call(with_sum(middle_kernel, 12, cid), grid_spec=pltpu.Prefetch...  36.4 us
    pallas_call x1, Pallas kernels, conv2_call(): pl.pallas_call(conv2_kernel, grid_spec=pltpu.PrefetchScalarGridSpec(num_s...  21.2 us
    pallas_call x1, Pallas kernels, conv1_call(): pl.pallas_call(with_sum(conv1_kernel, 9, cid), grid_spec=pltpu.PrefetchSc...  19.6 us

commit v1 on v0

--- a/solution.py
+++ b/solution.py
@@ -195,7 +195,7 @@
             g_refs, rest = rest[:m], rest[m:]
             mains, o_ref, rest = rest[:n_out], rest[n_out], rest[n_out + 1 :]
             own, sems = rest[:3], rest[3:]
-            start, advance, finish, rounds = scatter_steps(pieces, g_refs, o_ref, sems, 2)
+            start, advance, finish, rounds = scatter_steps(pieces, g_refs, o_ref, sems, 3)
             peers = link_peers(*place())
 
             @pl.when(at == 0)
@@ -348,7 +348,7 @@
     return [dma((n, NZ - 1)), dma((n, NZ - 1))] + [dma((n,))] * 6 + [dma((groups,))]
 
 
-LEAD = 3
+LEAD = 2
 
 
 def gather_events(pieces, xs, gs, sems):
@@ -908,10 +908,11 @@
 
 
 FRONT_PIECES = (
-    [(0, at + 256 * j, 256) for j in range(4) for at in (0, 1024)]
+    [(0, at + k, 128) for k in (0, 128) for at in (0, 1024)]
+    + [(0, at + 256 * j, 256) for j in range(1, 4) for at in (0, 1024)]
     + [(0, 2048 + 256 * k, 256) for k in range(4)]
-    + [(1, 256 * k, 256) for k in (2, 0, 1, 3)]
-    + [(2, at + 256 * j, 256) for j in range(4) for at in (0, 1024)]
+    + [(1, 0, 512), (1, 512, 512)]
+    + [(2, at + 512 * j, 512) for j in range(2) for at in (0, 1024)]
 )
 
 
@@ -1001,7 +1002,7 @@
 
             @pl.when(i == j)
             def _(j=j):
-                until(j)
+                until(j + 1)
 
         @pl.when(i < chunks)
         def _():
@@ -1030,13 +1031,13 @@
                 scaled, _ = ln_stats(first)
                 hn_s[here, :] = (scaled * row(vecs, 3) + row(vecs, 4)).astype(BF)
             copies[1].start()
-            until(chunks)
+            until(chunks + 1)
             part = width // 2
             for t in range(2):
                 c = slice(t * part, (t + 1) * part)
                 pos[:, c] = nn(table_ref[...], weight(t, SEG["pos"][0], part)).astype(BF)
             copies[6].start()
-            until(chunks + 1)
+            until(chunks + 2)
             copies[0].start()
             at = SEG["qkv"][0]
             @pl.loop(0, 2)
@@ -1062,7 +1063,7 @@
         base = order[done[0] - 1][0] + 6.0
         blocks = full // BLK
         spots = batch * pairs * blocks
-        slots = [min(max(int((now + 2.0 - base) / 0.9), 0), spots) for now, _, _ in left]
+        slots = [min(max(int((now + 5.0 - base) / 0.9), 0), spots) for now, _, _ in left]
 
         def hook(blk):
             for slot, (_, kind, pair) in zip(slots, left):

time: 299 us -> 296 us (0.990)
  Pallas kernels: 295 us -> 291 us
    pallas_call x1, Pallas kernels: 68.7 us -> 65.7 us  [attn_bwd_call(): pl.pallas_call(body, grid_spec=pltpu.PrefetchScalarGridSpec(num_scalar_pr...]
where the time goes in v1:
time: 296 us; the launch traced here: 295 us
  Pallas kernels  291 us (98%)
  local copies, waits for them, and re-layouts  3.32 us (1%)
    pallas_call x1, Pallas kernels, front_call(): pl.pallas_call(body, grid_spec=pltpu.PrefetchScalarGridSpec(num_scalar_pr...  91.4 us
    pallas_call x1, Pallas kernels, attn_bwd_call(): pl.pallas_call(body, grid_spec=pltpu.PrefetchScalarGridSpec(num_scalar_pr...  65.7 us
    pallas_call x1, Pallas kernels, last_call(): pl.pallas_call(body, grid=(blocks + chunks,), in_specs=in_specs, out_spec...  52.6 us
    pallas_call x1, Pallas kernels, middle_call(): pl.pallas_call(with_sum(middle_kernel, 12, cid), grid_spec=pltpu.Prefetch...  36.9 us
    pallas_call x1, Pallas kernels, conv2_call(): pl.pallas_call(conv2_kernel, grid_spec=pltpu.PrefetchScalarGridSpec(num_s...  21.2 us
    pallas_call x1, Pallas kernels, conv1_call(): pl.pallas_call(with_sum(conv1_kernel, 9, cid), grid_spec=pltpu.PrefetchSc...  17.9 us

profile of v1, /device:TPU:0, one launch (start us, length us, event | category | flops | bytes accessed | tf_op | source)
XLA Modules:
  0.0 295.5 jit_solution(3919007337267650074)
XLA Ops:
  0.6 0.0 copy-start
  0.7 0.7 copy-done
  1.3 0.7 dynamic-slice_reduce_fusion.len_ref.refs_0_.lens
  2.0 3.2 %prepare.1 = (bf16[32,3072]{1,0:T(8,128)(2,1)}, bf16[32,1024]{1,0:T(8,128)(2,1)}, bf16[32,2048]{1,0:T(8,128)(2,1)}, bf16[112,128]{1,0:T(8,128)(2,1)}, bf16[1024,512]{1,0:T(8,128)(2,1)}) custom-call(bf16[32,1024]{1,0:T(8,128)(2,1)} %f1i.1, bf16[32,1024]{1,0:T(8,128)(2,1)} %bitcast.59, bf16[32,256]{1,0:T(8,128)(2,1)} %pos.1, bf16[3,32,256]{2,1,0:T(8,128)(2,1)} %bitcast.61, ...), custom_call_target="tpu_custom_call" | custom-call | tf_op jit(solution)/shard_map/prepare/pallas_call | solution.py:532
  5.2 91.4 %front.1 = (bf16[2,4,2,2,32,3072]{5,4,3,2,1,0:T(8,128)(2,1)}, bf16[2,4,2,2,32,1024]{5,4,3,2,1,0:T(8,128)(2,1)}, bf16[2,4,2,2,32,2048]{5,4,3,2,1,0:T(8,128)(2,1)}...) custom-call(s32[2]{0:T(128)} %dynamic-slice_reduce_fusion.len_ref.re, ...), custom_call_target="tpu_custom_call" | custom-call | tf_op jit(solution)/shard_map/front/pallas_call | solution.py:1105
  96.6 17.9 %conv_forward.1 = (f32[1024,512]{1,0:T(8,128)}, bf16[1024,1024]{1,0:T(8,128)(2,1)}, f32[1024,512]{1,0:T(8,128)}, f32[8,512]{1,0:T(8,128)}) custom-call(s32[2]{0:T(128)} %dynamic-slice_reduce_fusion.len_ref.refs_0_.lens, bf16[1024,512]{1,0:T(8,128)(2,1)} %bitcast.43, f32[1024,512]{1,0:T(8,128)} %get-tuple-element.80.refs_2_.refs_3_, ...), custom_call_target="tpu_custom_call" | custom-call | tf_op jit(solution)/shard_map/conv_forward/pallas_call | solution.py:1233
  114.5 36.9 %conv_out_ffn2.1 = (bf16[1024,512]{1,0:T(8,128)(2,1)}, f32[1024,512]{1,0:T(8,128)}, f32[1024,512]{1,0:T(8,128)}, f32[8,512]{1,0:T(8,128)}, f32[40,512]{1,0:T(8,1...) custom-call(s32[2]{0:T(128)} %dynamic-slice_reduce_fusion.len_ref.refs_0_.lens, ...), custom_call_target="tpu_custom_call" | custom-call | tf_op jit(solution)/shard_map/conv_out_ffn2/pallas_call | solution.py:1374
  151.4 21.2 %conv_backward.1 = (f32[1024,512]{1,0:T(8,128)}, bf16[1024,512]{1,0:T(8,128)(2,1)}, f32[40,512]{1,0:T(8,128)}, bf16[2,512,512]{2,1,0:T(8,128)(2,1)}, bf16[2,512,256]{2,1,0:T(8,128)(2,1)}) custom-call(s32[2]{0:T(128)} %dynamic-slice_reduce_fusion.len_ref.refs_0_.lens, f32[1024,512]{1,0:T(8,128)} %get-tuple-element.94.dy, ...), custom_call_target="tpu_custom_call" | custom-call | tf_op jit(solution)/shard_map/conv_backward/pallas_call | solution.py:1485
  172.6 65.7 %attn_bwd.1 = (bf16[2,512,512]{2,1,0:T(8,128)(2,1)}, bf16[2,512,512]{2,1,0:T(8,128)(2,1)}, bf16[2,512,512]{2,1,0:T(8,128)(2,1)}, bf16[2,1024,512]{2,1,0:T(8,128)...) custom-call(s32[2]{0:T(128)} %dynamic-slice_reduce_fusion.len_ref.refs_0_.lens, ...), custom_call_target="tpu_custom_call" | custom-call | tf_op jit(solution)/shard_map/attn_bwd/pallas_call | solution.py:217
  238.3 0.0 copy-start.1
  238.3 52.6 %qkv_ffn1_backward.1 = (bf16[1024,512]{1,0:T(8,128)(2,1)}, f32[32,3072]{1,0:T(8,128)}, f32[48,512]{1,0:T(8,128)}) custom-call(bf16[1024,512]{1,0:T(8,128)(2,1)} %bitcast.52, bf16[1024,512]{1,0:T(8,128)(2,1)} %bitcast.53, bf16[1024,512]{1,0:T(8,128)(2,1)} %bitcast.54, f32[1024,512]{1,0:T(8,128)} %get-tuple-element.80.refs_2_.refs_3_, ...), custom_call_target="tpu_custom_call" | custom-call | tf_op jit(solution)/shard_map/qkv_ffn1_backward/pallas_call | solution.py:1739
  291.0 0.0 copy-start.2
  291.0 2.5 own_gradients.1
  293.5 0.0 copy-done.1
  293.5 1.0 copy.37
  294.5 0.0 copy-done.2
  294.5 1.0 copy.38
Async XLA Ops:
  0.6 0.7 copy-start
  238.3 55.2 %copy-start.1 = (bf16[1024,512]{1,0:T(8,128)(2,1)S(1)}, bf16[1024,512]{1,0:T(8,128)(2,1)}, u32[]{:S(2)}) copy-start(bf16[1024,512]{1,0:T(8,128)(2,1)} %get-tuple-element.87) | copy-start | bytes 3145732
  291.0 3.5 %copy-start.2 = (bf16[1024,512]{1,0:T(8,128)(2,1)S(1)}, bf16[1024,512]{1,0:T(8,128)(2,1)}, u32[]{:S(2)}) copy-start(bf16[1024,512]{1,0:T(8,128)(2,1)} %get-tuple-element.114) | copy-start | bytes 3145732

commit v2 on v1

--- a/solution.py
+++ b/solution.py
@@ -178,7 +178,7 @@
     body, params = attn_bwd_kernel, dense_params()
     if early is not None:
         items = [split_owners(item) for item in early]
-        pieces = pieces_of([item.shape[-1] for item in items])
+        pieces = pieces_of([item.shape[-1] for item in items], 512)
         owned = items[0].shape[-2]
         n_in, n_out, m = len(args) - 1, len(out_shape), len(items)
         args += items

time: 296 us -> 295 us (level)
  no operation moved by 1% of the time
where the time goes in v2:
time: 295 us
  Pallas kernels  291 us (99%)
  local copies, waits for them, and re-layouts  3.32 us (1%)
    pallas_call x1, Pallas kernels, front_call(): pl.pallas_call(body, grid_spec=pltpu.PrefetchScalarGridSpec(num_scalar_pr...  90.2 us
    pallas_call x1, Pallas kernels, attn_bwd_call(): pl.pallas_call(body, grid_spec=pltpu.PrefetchScalarGridSpec(num_scalar_pr...  66 us
    pallas_call x1, Pallas kernels, last_call(): pl.pallas_call(body, grid=(blocks + chunks,), in_specs=in_specs, out_spec...  52.7 us
    pallas_call x1, Pallas kernels, middle_call(): pl.pallas_call(with_sum(middle_kernel, 12, cid), grid_spec=pltpu.Prefetch...  36.1 us
    pallas_call x1, Pallas kernels, conv2_call(): pl.pallas_call(conv2_kernel, grid_spec=pltpu.PrefetchScalarGridSpec(num_s...  21.2 us
    pallas_call x1, Pallas kernels, conv1_call(): pl.pallas_call(with_sum(conv1_kernel, 9, cid), grid_spec=pltpu.PrefetchSc...  18.8 us

profile of v2, /device:TPU:0, one launch (start us, length us, event | category | flops | bytes accessed | tf_op | source)
XLA Modules:
  0.0 294.8 jit_solution(17263268007701012609)
XLA Ops:
  0.6 0.0 copy-start
  0.7 0.7 copy-done
  1.3 0.7 dynamic-slice_reduce_fusion.len_ref.refs_0_.lens
  2.0 3.2 %prepare.1 = (bf16[32,3072]{1,0:T(8,128)(2,1)}, bf16[32,1024]{1,0:T(8,128)(2,1)}, bf16[32,2048]{1,0:T(8,128)(2,1)}, bf16[112,128]{1,0:T(8,128)(2,1)}, bf16[1024,512]{1,0:T(8,128)(2,1)}) custom-call(bf16[32,1024]{1,0:T(8,128)(2,1)} %f1i.1, bf16[32,1024]{1,0:T(8,128)(2,1)} %bitcast.59, bf16[32,256]{1,0:T(8,128)(2,1)} %pos.1, bf16[3,32,256]{2,1,0:T(8,128)(2,1)} %bitcast.61, ...), custom_call_target="tpu_custom_call" | custom-call | tf_op jit(solution)/shard_map/prepare/pallas_call | solution.py:532
  5.2 90.2 %front.1 = (bf16[2,4,2,2,32,3072]{5,4,3,2,1,0:T(8,128)(2,1)}, bf16[2,4,2,2,32,1024]{5,4,3,2,1,0:T(8,128)(2,1)}, bf16[2,4,2,2,32,2048]{5,4,3,2,1,0:T(8,128)(2,1)}...) custom-call(s32[2]{0:T(128)} %dynamic-slice_reduce_fusion.len_ref.re, ...), custom_call_target="tpu_custom_call" | custom-call | tf_op jit(solution)/shard_map/front/pallas_call | solution.py:1105
  95.4 18.8 %conv_forward.1 = (f32[1024,512]{1,0:T(8,128)}, bf16[1024,1024]{1,0:T(8,128)(2,1)}, f32[1024,512]{1,0:T(8,128)}, f32[8,512]{1,0:T(8,128)}) custom-call(s32[2]{0:T(128)} %dynamic-slice_reduce_fusion.len_ref.refs_0_.lens, bf16[1024,512]{1,0:T(8,128)(2,1)} %bitcast.43, f32[1024,512]{1,0:T(8,128)} %get-tuple-element.80.refs_2_.refs_3_, ...), custom_call_target="tpu_custom_call" | custom-call | tf_op jit(solution)/shard_map/conv_forward/pallas_call | solution.py:1233
  114.3 36.1 %conv_out_ffn2.1 = (bf16[1024,512]{1,0:T(8,128)(2,1)}, f32[1024,512]{1,0:T(8,128)}, f32[1024,512]{1,0:T(8,128)}, f32[8,512]{1,0:T(8,128)}, f32[40,512]{1,0:T(8,1...) custom-call(s32[2]{0:T(128)} %dynamic-slice_reduce_fusion.len_ref.refs_0_.lens, ...), custom_call_target="tpu_custom_call" | custom-call | tf_op jit(solution)/shard_map/conv_out_ffn2/pallas_call | solution.py:1374
  150.4 21.2 %conv_backward.1 = (f32[1024,512]{1,0:T(8,128)}, bf16[1024,512]{1,0:T(8,128)(2,1)}, f32[40,512]{1,0:T(8,128)}, bf16[2,512,512]{2,1,0:T(8,128)(2,1)}, bf16[2,512,256]{2,1,0:T(8,128)(2,1)}) custom-call(s32[2]{0:T(128)} %dynamic-slice_reduce_fusion.len_ref.refs_0_.lens, f32[1024,512]{1,0:T(8,128)} %get-tuple-element.94.dy, ...), custom_call_target="tpu_custom_call" | custom-call | tf_op jit(solution)/shard_map/conv_backward/pallas_call | solution.py:1485
  171.7 66.0 %attn_bwd.1 = (bf16[2,512,512]{2,1,0:T(8,128)(2,1)}, bf16[2,512,512]{2,1,0:T(8,128)(2,1)}, bf16[2,512,512]{2,1,0:T(8,128)(2,1)}, bf16[2,1024,512]{2,1,0:T(8,128)...) custom-call(s32[2]{0:T(128)} %dynamic-slice_reduce_fusion.len_ref.refs_0_.lens, ...), custom_call_target="tpu_custom_call" | custom-call | tf_op jit(solution)/shard_map/attn_bwd/pallas_call | solution.py:217
  237.7 0.0 copy-start.1
  237.7 52.7 %qkv_ffn1_backward.1 = (bf16[1024,512]{1,0:T(8,128)(2,1)}, f32[32,3072]{1,0:T(8,128)}, f32[48,512]{1,0:T(8,128)}) custom-call(bf16[1024,512]{1,0:T(8,128)(2,1)} %bitcast.52, bf16[1024,512]{1,0:T(8,128)(2,1)} %bitcast.53, bf16[1024,512]{1,0:T(8,128)(2,1)} %bitcast.54, f32[1024,512]{1,0:T(8,128)} %get-tuple-element.80.refs_2_.refs_3_, ...), custom_call_target="tpu_custom_call" | custom-call | tf_op jit(solution)/shard_map/qkv_ffn1_backward/pallas_call | solution.py:1739
  290.4 0.0 copy-start.2
  290.4 2.5 own_gradients.1
  292.9 0.0 copy-done.1
  292.9 1.0 copy.37
  293.9 0.0 copy-done.2
  293.9 1.0 copy.38
Async XLA Ops:
  0.6 0.7 copy-start
  237.7 55.2 %copy-start.1 = (bf16[1024,512]{1,0:T(8,128)(2,1)S(1)}, bf16[1024,512]{1,0:T(8,128)(2,1)}, u32[]{:S(2)}) copy-start(bf16[1024,512]{1,0:T(8,128)(2,1)} %get-tuple-element.87) | copy-start | bytes 3145732
  290.4 3.5 %copy-start.2 = (bf16[1024,512]{1,0:T(8,128)(2,1)S(1)}, bf16[1024,512]{1,0:T(8,128)(2,1)}, u32[]{:S(2)}) copy-start(bf16[1024,512]{1,0:T(8,128)(2,1)} %get-tuple-element.114) | copy-start | bytes 3145732
